TPU v7x, 256 devices: a whole 4x4x8 slice. The times are simulated.
256 devices in a mesh: outer: 32 (over z_lo, x, core), inner: 8 (over y, z_hi).
Axes of the slice: x: 4, y: 4, z: 8 (z_hi: 2, z_lo: 4; z = z_hi * 4 + z_lo), core: 2. Of those that a mesh axis runs over, the one named last changes fastest.
Arguments:
- qkv: bfloat16 [16384, 8, 10, 128], P(('outer', 'inner')), may hold values from -96 to 96
- key_codes: int32 [4096, 8, 16], P('outer', 'inner'), may hold values from 0 to 255
- codebooks: bfloat16 [8, 256, 128], P('inner'), may hold values from -4 to 4
- value_codes: bfloat16 [4096, 8, 128], P('outer', 'inner'), may hold values from -4 to 4
- value_scales: float32 [4096, 8], P('outer', 'inner'), may hold values from 0.25 to 4
- block_ids: int32 [32], P('outer'), may hold values from 0 to 31, each once
Outputs:
- attended: bfloat16 [16384, 8, 8, 128], P(('outer', 'inner'))
All inputs are finite; a program needn't handle non-finite values.
Results may differ from a plain program's by a relative error of at most 0.011.
Values may be sent and summed in bfloat16 or wider, within the bound.
A program may use at most 64 MiB of HBM per device.

v0:
```python
import math

import jax
import jax.numpy as jnp
from jax import lax
from jax.sharding import PartitionSpec as P

rope_base = 500000.0


def rotate(tensor, position):
    half_dim = tensor.shape[-1] // 2
    ladder = jnp.arange(half_dim, dtype=jnp.float32)
    inverse = jnp.exp(ladder * jnp.float32(-2.0 * math.log(rope_base) / tensor.shape[-1]))
    angles = position.astype(jnp.float32)[:, None] * inverse[None, :]
    target = (position.shape[0],) + (1,) * (tensor.ndim - 2) + (half_dim,)
    cosine = jnp.cos(angles).reshape(target)
    sine_part = jnp.sin(angles).reshape(target)
    floats = tensor.astype(jnp.float32)
    first_half = floats[..., :half_dim]
    second_half = floats[..., half_dim:]
    return jnp.concatenate(
        [
            first_half * cosine - second_half * sine_part,
            second_half * cosine + first_half * sine_part,
        ],
        axis=-1,
    )


def decode_block(key_codes, codebooks):
    block_rows, kv_local, group_count = key_codes.shape
    entries = codebooks.shape[1]
    head_dim = codebooks.shape[2]
    ladder = lax.broadcasted_iota(jnp.int32, (1, 1, 1, entries), 3).astype(jnp.float32)
    one_hot = (key_codes.astype(jnp.float32)[..., None] == ladder).astype(jnp.bfloat16)
    code_table = codebooks.reshape(kv_local, entries, group_count, head_dim // group_count)
    decoded = jnp.einsum("bkgc,kcgd->bkgd", one_hot, code_table, preferred_element_type=jnp.float32)
    return decoded.reshape(block_rows, kv_local, head_dim)


def span_of():
    return 1024


def absorb(state, queries, key_rows, value_rows, allowed):
    running_max, running_sum, weighted = state
    scores = jnp.einsum(
        "tkgd,nkd->tkgn", queries, key_rows, preferred_element_type=jnp.float32
    ) * queries.shape[-1] ** (-0.5)
    if allowed is not None:
        scores = jnp.where(allowed[:, None, None, :], scores, -jnp.inf)
    new_max = jnp.maximum(running_max, jnp.max(scores, axis=-1))
    decay_factor = jnp.exp(running_max - new_max)
    weights = jnp.exp(scores - new_max[..., None])
    running_sum = running_sum * decay_factor + jnp.sum(weights, axis=-1)
    weighted = weighted * decay_factor[..., None] + jnp.einsum(
        "tkgn,nkd->tkgd",
        weights.astype(jnp.bfloat16),
        value_rows,
        preferred_element_type=jnp.float32,
    )
    return (new_max, running_sum, weighted)


def shards(qkv, key_codes, codebooks, value_codes, value_scales, block_ids):
    group_heads = qkv.shape[2] - 2
    head_dim = qkv.shape[3]
    block_rows = key_codes.shape[0]
    prefix_len = block_rows * lax.axis_size("outer")
    prefix_values = (value_codes.astype(jnp.float32) * value_scales[:, :, None]).astype(
        jnp.bfloat16
    )
    exchanged = lax.all_to_all(qkv, "inner", split_axis=1, concat_axis=0, tiled=True)
    stretch_rows = exchanged.shape[0]
    kv_local = exchanged.shape[1]
    local_pos = jnp.arange(stretch_rows, dtype=jnp.int32)
    stretch_pos = prefix_len + local_pos
    queries = rotate(exchanged[:, :, :group_heads, :], stretch_pos).astype(jnp.bfloat16)
    stretch_keys = rotate(exchanged[:, :, group_heads, :], stretch_pos).astype(jnp.bfloat16)
    stretch_values = exchanged[:, :, group_heads + 1, :]
    initial = (
        jnp.full((stretch_rows, kv_local, group_heads), -1e30, jnp.float32),
        jnp.zeros((stretch_rows, kv_local, group_heads), jnp.float32),
        jnp.zeros((stretch_rows, kv_local, group_heads, head_dim), jnp.float32),
    )
    own_pos = block_ids[0] * block_rows + jnp.arange(block_rows, dtype=jnp.int32)
    prefix_keys = rotate(decode_block(key_codes, codebooks), own_pos).astype(jnp.bfloat16)
    key_rows = lax.all_gather(prefix_keys, "outer", axis=0, tiled=True)
    value_rows = lax.all_gather(prefix_values, "outer", axis=0, tiled=True)
    length = key_rows.shape[0]
    span_rows = span_of()

    def advance(step_index, inner_state):
        first_row = step_index * span_rows
        key_part = lax.dynamic_slice_in_dim(key_rows, first_row, span_rows, 0)
        value_part = lax.dynamic_slice_in_dim(value_rows, first_row, span_rows, 0)
        return absorb(inner_state, queries, key_part, value_part, None)

    allowed = local_pos[None, :] <= local_pos[:, None]
    final_state = absorb(
        lax.fori_loop(0, length // span_rows, advance, initial),
        queries,
        stretch_keys,
        stretch_values,
        allowed,
    )
    running_max, running_sum, weighted = final_state
    outputs = (weighted / running_sum[..., None]).astype(jnp.bfloat16)
    return lax.all_to_all(outputs, "inner", split_axis=0, concat_axis=1, tiled=True)


def solution(mesh):
    return jax.shard_map(
        shards,
        mesh=mesh,
        in_specs=(
            P(("outer", "inner"), None, None, None),
            P("outer", "inner", None),
            P("inner", None, None),
            P("outer", "inner", None),
            P("outer", "inner"),
            P("outer"),
        ),
        out_specs=P(("outer", "inner"), None, None, None),
        check_vma=False,
    )
```

profile of v0, /device:TPU:32, one launch (start us, length us, event | category | flops | bytes accessed | tf_op | source)
XLA Modules:
  0.0 320.7 jit_solution(219991064677124452)
XLA Ops:
  6.6 0.8 convert_bitcast_fusion
  7.4 0.9 copy.48
  10.3 1.4 copy.49
  11.8 10.2 %all-to-all-start = ((bf16[64,8,10,128]{3,0,2,1:T(8,128)(2,1)}), bf16[64,8,10,128]{3,0,2,1:T(8,128)(2,1)S(1)}, u32[]{:S(2)}, u32[]{:S(2)}) async-start(bf16[64,8,10,128]{3,0,2,1:T(8,128)(2,1)} %copy.49), calls=%async_computation | async-start | bytes 2621440 | tf_op jit(solution)/shard_map/all_to_all | solution.py:74
  22.8 0.8 iota_compare_fusion
  23.6 1.8 multiply_cosine_fusion.1
  25.4 35.3 %all-to-all-done = bf16[64,8,10,128]{3,0,2,1:T(8,128)(2,1)S(1)} async-done(((bf16[64,8,10,128]{3,0,2,1:T(8,128)(2,1)}), bf16[64,8,10,128]{3,0,2,1:T(8,128)(2,1)S(1)}, u32[]{:S(2)}, u32[]{:S(2)}) %all-to-all-start) | async-done | bytes 1310752 | tf_op jit(solution)/shard_map/all_to_all | solution.py:74
  61.0 1.0 copy-done.7
  62.2 0.8 subtract_convert_fusion
  63.0 0.9 copy-done
  65.3 25.1 %all-gather.3.cloned.1.call-done = bf16[4096,1,128]{0,2,1:T(8,128)(2,1)} async-done(((bf16[128,1,128]{0,2,1:T(8,128)(2,1)}), bf16[4096,1,128]{0,2,1:T(8,128)(2,1)}) %all-gather.3.cloned.1.call-update) | async-done | bytes 1048592 | tf_op jit(solution)/shard_map/all_gather | solution.py:89
  90.4 67.9 %all-gather.5.cloned.1.call-done = bf16[4096,1,128]{0,2,1:T(8,128)(2,1)} async-done(((bf16[128,1,128]{0,2,1:T(8,128)(2,1)}), bf16[4096,1,128]{0,2,1:T(8,128)(2,1)}) %all-gather.5.cloned.1.call-update) | async-done | bytes 1048592 | tf_op jit(solution)/shard_map/all_gather | solution.py:90
  158.4 101.3 %while.18 = (s32[]{:T(128)}, f32[512,1,8]{0,2,1:T(8,128)S(1)}, f32[512,1,8]{0,2,1:T(8,128)S(1)}, f32[512,1,8,128]{0,3,2,1:T(8,128)S(1)}, bf16[4096,1,128]{0,2,1:...) while((s32[]{:T(128)}, f32[512,1,8]{0,2,1:T(8,128)S(1)}, ...), condition=%wide.region_3.0_spmd.clone, body=%wide.region_0.0_spmd.clone.sunk | while | flops 2182635520 | bytes 56361140 | solution.py:102
  158.4 9.1 %bitcast_reduce_fusion.2 = (f32[512,8]{0,1:T(8,128)S(1)}, f32[1024,512,8]{1,0,2:T(8,128)}) fusion(bf16[512,1,8,128]{3,0,2,1:T(8,128)(2,1)S(1)} %get-tuple-element.273, bf16[4096,1,128]{0,2,1:T(8,128)(2,1)} %get-tuple-element.272, s32[]{:T(128)S(6)} %select_n.27), kind=kOutput, calls=%fused_computation.1.clone.1 | convolution fusion | flops 1082126336 | bytes 18104324 | tf_op jit(solution)/shard_map/while/body/eval_jaxpr/tkgd,nkd->tkgn/dot_general | solution.py:48
  167.5 8.5 %fusion.77 = f32[512,8]{0,1:T(8,128)S(1)} fusion(f32[1024,512,8]{1,0,2:T(8,128)} %get-tuple-element.244, f32[512,8]{0,1:T(8,128)S(1)} %bitcast.167), kind=kLoop, calls=%fused_computation.4.clone.1 | loop fusion | flops 12578816 | bytes 16809984 | tf_op jit(solution)/shard_map/while/body/eval_jaxpr/reduce_sum | solution.py:56
  176.0 7.7 %bitcast_add_fusion.7 = f32[512,1,8,128]{0,3,2,1:T(8,128)S(1)} fusion(f32[512,1,8,128]{0,3,2,1:T(8,128)S(1)} %get-tuple-element.260, f32[1024,512,8]{1,0,2:T(8,128)} %get-tuple-element.244, f32[512,8]{0,1:T(8,128)S(1)} %bitcast.168, f32[512,8]{0,1:T(8,128)S(1)} %get-tuple-element.245, pred[]{:T(512)S(6)} %compare.3, ...), kind=kOutput, calls=%fused_computation.9.clone.1 | convolution fusion | flops 1087897600 | bytes 21266436 | tf_op jit(solution)/shard_map/while/body/eval_jaxpr/tkgn,nkd->tkgd/dot_general | solution.py:57
  183.7 9.1 %bitcast_reduce_fusion.2 = (f32[512,8]{0,1:T(8,128)S(1)}, f32[1024,512,8]{1,0,2:T(8,128)}) fusion(bf16[512,1,8,128]{3,0,2,1:T(8,128)(2,1)S(1)} %get-tuple-element.273, bf16[4096,1,128]{0,2,1:T(8,128)(2,1)} %get-tuple-element.272, s32[]{:T(128)S(6)} %select_n.27), kind=kOutput, calls=%fused_computation.1.clone.1 | convolution fusion | flops 1082126336 | bytes 18104324 | tf_op jit(solution)/shard_map/while/body/eval_jaxpr/tkgd,nkd->tkgn/dot_general | solution.py:48
  192.8 8.5 %fusion.77 = f32[512,8]{0,1:T(8,128)S(1)} fusion(f32[1024,512,8]{1,0,2:T(8,128)} %get-tuple-element.244, f32[512,8]{0,1:T(8,128)S(1)} %bitcast.167), kind=kLoop, calls=%fused_computation.4.clone.1 | loop fusion | flops 12578816 | bytes 16809984 | tf_op jit(solution)/shard_map/while/body/eval_jaxpr/reduce_sum | solution.py:56
  201.3 7.7 %bitcast_add_fusion.7 = f32[512,1,8,128]{0,3,2,1:T(8,128)S(1)} fusion(f32[512,1,8,128]{0,3,2,1:T(8,128)S(1)} %get-tuple-element.260, f32[1024,512,8]{1,0,2:T(8,128)} %get-tuple-element.244, f32[512,8]{0,1:T(8,128)S(1)} %bitcast.168, f32[512,8]{0,1:T(8,128)S(1)} %get-tuple-element.245, pred[]{:T(512)S(6)} %compare.3, ...), kind=kOutput, calls=%fused_computation.9.clone.1 | convolution fusion | flops 1087897600 | bytes 21266436 | tf_op jit(solution)/shard_map/while/body/eval_jaxpr/tkgn,nkd->tkgd/dot_general | solution.py:57
  209.0 9.1 %bitcast_reduce_fusion.2 = (f32[512,8]{0,1:T(8,128)S(1)}, f32[1024,512,8]{1,0,2:T(8,128)}) fusion(bf16[512,1,8,128]{3,0,2,1:T(8,128)(2,1)S(1)} %get-tuple-element.273, bf16[4096,1,128]{0,2,1:T(8,128)(2,1)} %get-tuple-element.272, s32[]{:T(128)S(6)} %select_n.27), kind=kOutput, calls=%fused_computation.1.clone.1 | convolution fusion | flops 1082126336 | bytes 18104324 | tf_op jit(solution)/shard_map/while/body/eval_jaxpr/tkgd,nkd->tkgn/dot_general | solution.py:48
  218.1 8.5 %fusion.77 = f32[512,8]{0,1:T(8,128)S(1)} fusion(f32[1024,512,8]{1,0,2:T(8,128)} %get-tuple-element.244, f32[512,8]{0,1:T(8,128)S(1)} %bitcast.167), kind=kLoop, calls=%fused_computation.4.clone.1 | loop fusion | flops 12578816 | bytes 16809984 | tf_op jit(solution)/shard_map/while/body/eval_jaxpr/reduce_sum | solution.py:56
  226.7 7.7 %bitcast_add_fusion.7 = f32[512,1,8,128]{0,3,2,1:T(8,128)S(1)} fusion(f32[512,1,8,128]{0,3,2,1:T(8,128)S(1)} %get-tuple-element.260, f32[1024,512,8]{1,0,2:T(8,128)} %get-tuple-element.244, f32[512,8]{0,1:T(8,128)S(1)} %bitcast.168, f32[512,8]{0,1:T(8,128)S(1)} %get-tuple-element.245, pred[]{:T(512)S(6)} %compare.3, ...), kind=kOutput, calls=%fused_computation.9.clone.1 | convolution fusion | flops 1087897600 | bytes 21266436 | tf_op jit(solution)/shard_map/while/body/eval_jaxpr/tkgn,nkd->tkgd/dot_general | solution.py:57
  234.4 9.1 %bitcast_reduce_fusion.2 = (f32[512,8]{0,1:T(8,128)S(1)}, f32[1024,512,8]{1,0,2:T(8,128)}) fusion(bf16[512,1,8,128]{3,0,2,1:T(8,128)(2,1)S(1)} %get-tuple-element.273, bf16[4096,1,128]{0,2,1:T(8,128)(2,1)} %get-tuple-element.272, s32[]{:T(128)S(6)} %select_n.27), kind=kOutput, calls=%fused_computation.1.clone.1 | convolution fusion | flops 1082126336 | bytes 18104324 | tf_op jit(solution)/shard_map/while/body/eval_jaxpr/tkgd,nkd->tkgn/dot_general | solution.py:48
  243.5 8.5 %fusion.77 = f32[512,8]{0,1:T(8,128)S(1)} fusion(f32[1024,512,8]{1,0,2:T(8,128)} %get-tuple-element.244, f32[512,8]{0,1:T(8,128)S(1)} %bitcast.167), kind=kLoop, calls=%fused_computation.4.clone.1 | loop fusion | flops 12578816 | bytes 16809984 | tf_op jit(solution)/shard_map/while/body/eval_jaxpr/reduce_sum | solution.py:56
  252.0 7.7 %bitcast_add_fusion.7 = f32[512,1,8,128]{0,3,2,1:T(8,128)S(1)} fusion(f32[512,1,8,128]{0,3,2,1:T(8,128)S(1)} %get-tuple-element.260, f32[1024,512,8]{1,0,2:T(8,128)} %get-tuple-element.244, f32[512,8]{0,1:T(8,128)S(1)} %bitcast.168, f32[512,8]{0,1:T(8,128)S(1)} %get-tuple-element.245, pred[]{:T(512)S(6)} %compare.3, ...), kind=kOutput, calls=%fused_computation.9.clone.1 | convolution fusion | flops 1087897600 | bytes 21266436 | tf_op jit(solution)/shard_map/while/body/eval_jaxpr/tkgn,nkd->tkgd/dot_general | solution.py:57
  259.7 1.8 copy.53
  261.5 2.4 fusion.54
  263.9 3.4 %fusion.22 = (f32[512,8]{0,1:T(8,128)S(1)}, f32[512,512,8]{1,0,2:T(8,128)S(1)}) fusion(pred[512,512]{0,1:T(8,128)(4,1)S(1)} %copy-done.4, bf16[512,8,64]{2,0,1:T(8,128)(2,1)} %bitcast.170, bf16[512,8,64]{2,0,1:T(8,128)(2,1)S(1)} %bitcast.169, bf16[512,64]{1,0:T(8,128)(2,1)S(1)} %get-tuple-element.186, bf16[512,64]{1,0:T(8,128)(2,1)S(1)} %get-tuple-element.185), kind=kOutput, calls=%fused_computation.29 | convolution fusion | flops 545517568 | bytes 9846784 | tf_op jit(solution)/shard_map/tkgd,nkd->tkgn/dot_general | solution.py:48
  267.4 1.7 fusion.20
  269.2 4.1 %fusion.28 = bf16[512,1,8,128]{3,0,2,1:T(8,128)(2,1)S(1)} fusion(f32[512,1,8,128]{3,0,2,1:T(8,128)S(1)} %copy-done.5, f32[512,512,8]{1,0,2:T(8,128)S(1)} %get-tuple-element.194, f32[512,8]{0,1:T(8,128)S(1)} %fusion.65, pred[512,512]{0,1:T(8,128)(4,1)S(1)} %copy-done.4, f32[512,8]{0,1:T(8,128)S(1)} %get-tuple-element.190, ...), kind=kOutput, calls=%fused_computation.35 | convolution fusion | flops 547356672 | bytes 11976704 | tf_op jit(solution)/shard_map/tkgn,nkd->tkgd/dot_general | solution.py:57
  274.0 38.6 %all_to_all.36 = bf16[512,1,8,128]{3,2,1,0:T(8,128)(2,1)S(1)} all-to-all(bf16[512,1,8,128]{3,2,1,0:T(8,128)(2,1)S(1)} %copy.55), channel_id=1, replica_groups=mesh['outer'=32,'inner'=8] {'inner'}, dimensions={0} | all-to-all | bytes 2097152 | tf_op jit(solution)/shard_map/all_to_all | solution.py:110
  312.6 1.3 copy.61
  (55 shorter events, 4.8 us)
Async XLA Ops:
  6.5 3.8 %copy-start.6 = (bf16[64,8,10,128]{3,1,2,0:T(8,128)(2,1)S(1)}, bf16[64,8,10,128]{3,1,2,0:T(8,128)(2,1)}, u32[]{:S(2)}) copy-start(bf16[64,8,10,128]{3,1,2,0:T(8,128)(2,1)} %param.8) | copy-start | bytes 3932164
  6.5 83.9 %all-gather.3.cloned.1.call-start = ((), (), s32[]{:S(2)}) async-start(), calls=%async_computation.2 | async-start | bytes 1081344 | tf_op jit(solution)/shard_map/all_gather | solution.py:89
  10.3 11.7 %copy-start.9 = (bf16[128,1,128]{2,0,1:T(8,128)(2,1)S(1)}, bf16[128,1,128]{2,0,1:T(8,128)(2,1)}, u32[]{:S(2)}) copy-start(bf16[128,1,128]{2,0,1:T(8,128)(2,1)} %param.11) | copy-start | bytes 98308
  10.3 11.8 %copy-start.10 = (f32[128,1]{0,1:T(1,128)S(1)}, f32[128,1]{0,1:T(1,128)}, u32[]{:S(2)}) copy-start(f32[128,1]{0,1:T(1,128)} %param.12) | copy-start | bytes 1540
  11.8 48.9 %all-to-all-start = ((bf16[64,8,10,128]{3,0,2,1:T(8,128)(2,1)}), bf16[64,8,10,128]{3,0,2,1:T(8,128)(2,1)S(1)}, u32[]{:S(2)}, u32[]{:S(2)}) async-start(bf16[64,8,10,128]{3,0,2,1:T(8,128)(2,1)} %copy.49), calls=%async_computation | async-start | bytes 2621440 | tf_op jit(solution)/shard_map/all_to_all | solution.py:74
  22.0 136.4 %all-gather.5.cloned.1.call-start = ((), (), s32[]{:S(2)}) async-start(), calls=%async_computation.3 | async-start | bytes 1081344 | tf_op jit(solution)/shard_map/all_gather | solution.py:90
  60.8 3.7 %copy-start.3 = (bf16[8,64,1,10,128]{4,1,0,3,2:T(8,128)(2,1)}, bf16[8,64,1,10,128]{4,1,0,3,2:T(8,128)(2,1)S(1)}, u32[]{:S(2)}) copy-start(bf16[8,64,1,10,128]{4,1,0,3,2:T(8,128)(2,1)S(1)} %copy.50) | copy-start | bytes 3932164
  60.8 1.1 copy-start.7
  60.8 1.4 copy-start.8
  63.0 1.0 copy-start
  63.0 1.6 copy-start.2
  259.7 4.2 %copy-start.1 = (bf16[512,1,8,64]{3,0,2,1:T(8,128)(2,1)S(1)}, bf16[512,1,8,64]{3,0,2,1:T(8,128)(2,1)}, u32[]{:S(2)}) copy-start(bf16[512,1,8,64]{3,0,2,1:T(8,128)(2,1)} %copy-done) | copy-start | bytes 1572868
  259.7 4.2 %copy-start.4 = (pred[512,512]{0,1:T(8,128)(4,1)S(1)}, pred[512,512]{0,1:T(8,128)(4,1)}, u32[]{:S(2)}) copy-start(pred[512,512]{0,1:T(8,128)(4,1)} %iota_compare_fusion) | copy-start | bytes 786436
  267.4 1.8 copy-start.5
Sparse Core Ops, SparseCore 0:
  10.4 79.9 all-gather.2
  92.2 66.1 all-gather.4
where the time goes:
time: 321 us
  waiting for transfers between devices  128 us (40%)
  matrix products  75.1 us (23%)
  other arithmetic  45.3 us (14%)
  blocking collectives  38.6 us (12%)
  between operations  14.3 us (4%)
  starting transfers between devices  10.2 us (3%)
  local copies, waits for them, and re-layouts  8.6 us (3%)
    all_gather x1, waiting for transfers between devices, shards(): value_rows = lax.all_gather(prefix_values, 'outer', axis=0, tiled=True)  67.9 us
    dot_general x5, matrix products, absorb(): jnp.einsum('tkgd,nkd->tkgn', queries, key_rows, preferred_element_type=jn...  39.8 us
    all_to_all x1, blocking collectives, shards(): lax.all_to_all(outputs, 'inner', split_axis=0, concat_axis=1, tiled=True)  38.6 us
    reduce_sum x5, other arithmetic, absorb(): running_sum = running_sum * decay_factor + jnp.sum(weights, axis=-1)  35.7 us
    all_to_all x1, waiting for transfers between devices, shards(): lax.all_to_all(qkv, 'inner', split_axis=1, concat_axis=0, tiled=True)  35.3 us
    dot_general x5, matrix products, absorb(): jnp.einsum('tkgn,nkd->tkgd', weights.astype(jnp.bfloat16), value_rows, pr...  34.8 us
    all_gather x1, waiting for transfers between devices, shards(): key_rows = lax.all_gather(prefix_keys, 'outer', axis=0, tiled=True)  25.1 us
    all_to_all x1, starting transfers between devices, shards(): lax.all_to_all(qkv, 'inner', split_axis=1, concat_axis=0, tiled=True)  10.2 us
  transfers between devices with their start and end apart: 3, of which 3 were waited for; matrix products, arithmetic and copies ran while one was open for 2% of the time, Pallas kernels for 0%

commit v1 on v0

v1 whole, which is shorter than its diff:
```python
import functools
import math

import jax
import jax.numpy as jnp
from jax import lax
from jax.experimental import pallas as pl
from jax.experimental.pallas import tpu as pltpu
from jax.sharding import PartitionSpec as P

rope_base = 500000.0
NX, NY, NZ, NH = 4, 4, 8, 4
BLOCK, HEAD, GQ, LOCAL = 128, 128, 8, 64
ROWS = 256
SCALE = 128**-0.5 * math.log2(math.e)
NT = (((1,), (1,)), ((), ()))


def rotate(tensor, position):
    half_dim = tensor.shape[-1] // 2
    ladder = jnp.arange(half_dim, dtype=jnp.float32)
    inverse = jnp.exp(ladder * jnp.float32(-2.0 * math.log(rope_base) / tensor.shape[-1]))
    angles = position.astype(jnp.float32)[:, None] * inverse[None, :]
    target = (position.shape[0],) + (1,) * (tensor.ndim - 2) + (half_dim,)
    cosine = jnp.cos(angles).reshape(target)
    sine_part = jnp.sin(angles).reshape(target)
    floats = tensor.astype(jnp.float32)
    first_half = floats[..., :half_dim]
    second_half = floats[..., half_dim:]
    return jnp.concatenate(
        [
            first_half * cosine - second_half * sine_part,
            second_half * cosine + first_half * sine_part,
        ],
        axis=-1,
    )


def decode_block(key_codes, codebooks):
    block_rows, kv_local, group_count = key_codes.shape
    entries = codebooks.shape[1]
    head_dim = codebooks.shape[2]
    ladder = lax.broadcasted_iota(jnp.int32, (1, 1, 1, entries), 3).astype(jnp.float32)
    one_hot = (key_codes.astype(jnp.float32)[..., None] == ladder).astype(jnp.bfloat16)
    code_table = codebooks.reshape(kv_local, entries, group_count, head_dim // group_count)
    decoded = jnp.einsum("bkgc,kcgd->bkgd", one_hot, code_table, preferred_element_type=jnp.float32)
    return decoded.reshape(block_rows, kv_local, head_dim)


def kernel(q_in, sk_in, sv_in, kv_in, out, kv, qb, sk, sv, rk, rv, ob, sa, sb, ma, mb,
           send, rs, rq, rsk, rsv, rrk, rrv, rx, ro, loc, osend):
    o = lax.axis_index("outer")
    i = lax.axis_index("inner")
    zl, x, c = o // 8, (o // 2) % NX, o % 2
    y, zh = i // 2, i % 2
    z = zh * NH + zl

    def dev(dx=0, dy=0, dz=0, dc=0):
        x1, y1, z1, c1 = (x + dx) % NX, (y + dy) % NY, (z + dz) % NZ, (c + dc) % 2
        return {"outer": (z1 % NH) * 8 + x1 * 2 + c1, "inner": y1 * 2 + z1 // NH}

    def slot(dz, dx, dc=0):
        return (((z + dz) % NZ) * NX + (x + dx) % NX) * 2 + (c + dc) % 2

    peers = [dev(dz=1), dev(dz=-1), dev(dx=1), dev(dx=-1), dev(dc=1)]
    peers += [dev(dy=d) for d in (1, 2, 3)]
    peers += [dev(dy=d, dz=s) for d in range(4) for s in (2, -2)]
    barrier = pltpu.get_barrier_semaphore()
    for peer in peers:
        pl.semaphore_signal(barrier, inc=1, device_id=peer, device_id_type=pl.DeviceIdType.MESH)
    pl.semaphore_wait(barrier, len(peers))

    sent = []

    def put(src, dst, recv_sem, to):
        copy = pltpu.make_async_remote_copy(
            src_ref=src, dst_ref=dst, send_sem=send.at[len(sent)], recv_sem=recv_sem,
            device_id=to, device_id_type=pl.DeviceIdType.MESH)
        copy.start()
        sent.append(copy)

    def got(dst, recv_sem):
        pltpu.make_async_copy(dst, dst, recv_sem).wait()

    kept = []

    def keep(src, dst):
        copy = pltpu.make_async_copy(src, dst, loc.at[len(kept)])
        copy.start()
        kept.append(copy)

    own = slot(0, 0)
    for to in (dev(dz=1), dev(dz=-1), dev(dx=1), dev(dx=-1), dev(dc=1)):
        put(kv_in, kv.at[own], rs.at[own, 0], to)
    keep(kv_in, kv.at[own])
    for d in range(4):
        yd = (y + d) % NY
        pair = pl.ds(2 * yd, 2)
        put(sk_in.at[pair], rk.at[y], rrk.at[y], dev(dy=d, dz=2))
        put(sv_in.at[pair], rv.at[y], rrv.at[y], dev(dy=d, dz=-2))
        if d == 0:
            keep(sk_in.at[pair], sk.at[zh, y])
            keep(sv_in.at[pair], sv.at[zh, y])
        else:
            put(sk_in.at[pair], sk.at[zh, y], rsk.at[y], dev(dy=d))
            put(sv_in.at[pair], sv.at[zh, y], rsv.at[y], dev(dy=d))
    for hh in (zh, 1 - zh):
        for d in range(4):
            yd = (y + d) % NY
            if d == 0:
                keep(q_in.at[2 * yd + hh], qb.at[hh, y])
            else:
                put(q_in.at[2 * yd + hh], qb.at[hh, y], rq.at[hh, y], dev(dy=d))

    def spread(s):
        put(kv.at[s], kv.at[s], rs.at[s, 0], dev(dx=1))
        put(kv.at[s], kv.at[s], rs.at[s, 0], dev(dx=-1))
        put(kv.at[s], kv.at[s], rs.at[s, 0], dev(dc=1))

    for d in (1, 2, 3):
        for sign in (-1, 1):
            s = slot(sign * d, 0)
            got(kv.at[s], rs.at[s, 0])
            if d < 3:
                put(kv.at[s], kv.at[s], rs.at[s, 0], dev(dz=-sign))
            else:
                half = 0 if sign < 0 else 1
                put(kv.at[s, half], kv.at[s, half], rs.at[s, half], dev(dz=-sign))
            spread(s)
    s = slot(4, 0)
    got(kv.at[s, 0], rs.at[s, 0])
    got(kv.at[s, 1], rs.at[s, 1])
    spread(s)

    for src in range(NY):
        got(rk.at[src], rrk.at[src])
        got(rv.at[src], rrv.at[src])
    put(rk, sk.at[((z + 6) % NZ) // NH], rx.at[0], dev(dz=2))
    put(rv, sv.at[((z + 2) % NZ) // NH], rx.at[1], dev(dz=-2))

    order = (0, -1, 1, -2, 2, -3, 3, 4)
    for dz in order:
        for sign in (-1, 1):
            s = slot(dz, sign)
            got(kv.at[s], rs.at[s, 0])
            half = 0 if sign < 0 else 1
            put(kv.at[s, half], kv.at[s, half], rs.at[s, half], dev(dx=-sign))
            put(kv.at[s], kv.at[s], rs.at[s, 0], dev(dc=1))
    for dz in order:
        s = slot(dz, 2)
        got(kv.at[s, 0], rs.at[s, 0])
        got(kv.at[s, 1], rs.at[s, 1])
        put(kv.at[s], kv.at[s], rs.at[s, 0], dev(dc=1))
    for dz in order:
        for dx in range(4):
            s = slot(dz, dx, 1)
            got(kv.at[s], rs.at[s, 0])
    for d in (1, 2, 3):
        src = (y + d) % NY
        got(sk.at[zh, src], rsk.at[src])
        got(sv.at[zh, src], rsv.at[src])
        for hh in range(2):
            got(qb.at[hh, src], rq.at[hh, src])
    got(sk.at[1 - zh], rx.at[0])
    got(sv.at[1 - zh], rx.at[1])
    for copy in kept:
        copy.wait()

    def unit(u):
        return (zh + u // 4) % 2, (y + 1 + u % 4) % NY

    def keys_of(hh, n):
        if n < 8:
            part = kv[pl.ds(hh * 32 + 4 * n, 4), 0]
            return part.reshape(4 * BLOCK, HEAD)
        return sk[n - 8, :, hh].reshape(4 * LOCAL, HEAD)

    def values_of(hh, n):
        if n < 8:
            part = kv[pl.ds(hh * 32 + 4 * n, 4), 1]
            return part.reshape(4 * BLOCK, HEAD)
        return sv[n - 8, :, hh].reshape(4 * LOCAL, HEAD)

    spans = [(512 * n, 512) for n in range(8)] + [(4096, 256), (4352, 256)]

    def query_tile(t):
        hh, src = unit(t // 2)
        floats = qb[hh, src, pl.ds(pl.multiple_of((t % 2) * ROWS, ROWS), ROWS), :].astype(jnp.float32) * SCALE
        high = floats.astype(jnp.bfloat16)
        low = (floats - high.astype(jnp.float32)).astype(jnp.bfloat16)
        return jnp.concatenate([high, low], axis=1)

    def score(t, n, buf):
        hh, src = unit(t // 2)
        keys = keys_of(hh, n)
        first, size = spans[n]
        keys = jnp.concatenate([keys, keys], axis=1)
        s = lax.dot_general(query_tile(t), keys, NT, preferred_element_type=jnp.float32)
        if n >= 8:
            token = (2 * src + zh) * LOCAL + (t % 2) * (ROWS // GQ)
            row = token + lax.broadcasted_iota(jnp.int32, (ROWS, size), 0) // GQ
            col = lax.broadcasted_iota(jnp.int32, (ROWS, size), 1)
            col = (col // LOCAL) * (2 * LOCAL) + (n - 8) * LOCAL + col % LOCAL
            s = jnp.where(col <= row, s, -1e30)
        buf[:, first:first + size] = s
        top = s[:, :128]
        for j in range(1, size // 128):
            top = jnp.maximum(top, s[:, j * 128:(j + 1) * 128])
        return top

    def weigh(t, n, buf, top):
        hh, _ = unit(t // 2)
        first, size = spans[n]
        weights = jnp.exp2(buf[:, first:first + size] - top).astype(jnp.bfloat16)
        values = values_of(hh, n)
        values = jnp.concatenate([values, jnp.ones_like(values)], axis=1)
        return jnp.dot(weights, values, preferred_element_type=jnp.float32)

    def stage(tn, bufn, mn, tc, bufc, mc):
        top, total = None, None
        for n in range(len(spans)):
            if tn is not None:
                part = score(tn, n, bufn)
                top = part if top is None else jnp.maximum(top, part)
            if tc is not None:
                part = weigh(tc, n, bufc, mc[:, :1])
                total = part if total is None else total + part
        if tn is not None:
            mn[...] = jnp.broadcast_to(jnp.max(top, axis=1, keepdims=True), mn.shape)
        if tc is not None:
            hh, src = unit(tc // 2)
            result = (total[:, :HEAD] / total[:, HEAD:]).reshape(ROWS // GQ, GQ, HEAD)
            at = pl.ds(pl.multiple_of((tc % 2) * (ROWS // GQ), ROWS // GQ), ROWS // GQ)
            ob[hh, src, at] = result.astype(jnp.bfloat16)

    def result_copy(u):
        hh, src = unit(u)
        return pltpu.make_async_remote_copy(
            src_ref=ob.at[hh, src], dst_ref=out.at[:, 2 * y + hh],
            send_sem=osend.at[u], recv_sem=ro.at[hh, y],
            device_id={"outer": o, "inner": src * 2 + zh}, device_id_type=pl.DeviceIdType.MESH)

    def own_copy(u):
        hh, src = unit(u)
        return pltpu.make_async_copy(ob.at[hh, src], out.at[:, 2 * y + hh], osend.at[u])

    stage(0, sa, ma, None, None, None)

    def body(u, carry):
        stage(2 * u + 1, sb, mb, 2 * u, sa, ma)
        stage(jnp.minimum(2 * u + 2, 15), sa, ma, 2 * u + 1, sb, mb)

        @pl.when(u % 4 < 3)
        def _():
            result_copy(u).start()

        @pl.when(u % 4 == 3)
        def _():
            own_copy(u).start()

        return carry

    lax.fori_loop(0, 8, body, 0)

    for copy in sent:
        copy.wait_send()
    for u in range(8):
        if u % 4 == 3:
            own_copy(u).wait()
        else:
            result_copy(u).wait_send()
    for hh in range(2):
        for d in (1, 2, 3):
            src = (y + d) % NY
            got(out.at[:, 2 * src + hh], ro.at[hh, src])


def shards(qkv, key_codes, codebooks, value_codes, value_scales, block_ids):
    block_rows = key_codes.shape[0]
    prefix_len = block_rows * lax.axis_size("outer")
    prefix_values = (value_codes.astype(jnp.float32) * value_scales[:, :, None]).astype(jnp.bfloat16)
    own_pos = block_ids[0] * block_rows + jnp.arange(block_rows, dtype=jnp.int32)
    prefix_keys = rotate(decode_block(key_codes, codebooks), own_pos).astype(jnp.bfloat16)
    kv_in = jnp.stack([prefix_keys[:, 0], prefix_values[:, 0]])
    stretch_pos = prefix_len + lax.axis_index("inner") * LOCAL + jnp.arange(LOCAL, dtype=jnp.int32)
    rotated = rotate(qkv[:, :, :GQ + 1], stretch_pos).astype(jnp.bfloat16)
    q_in = rotated[:, :, :GQ].transpose(1, 0, 2, 3).reshape(8, LOCAL * GQ, HEAD)
    sk_in = rotated[:, :, GQ].transpose(1, 0, 2)
    sv_in = qkv[:, :, GQ + 1].transpose(1, 0, 2)

    bf, f32 = jnp.bfloat16, jnp.float32
    dma = pltpu.SemaphoreType.DMA
    return pl.pallas_call(
        kernel,
        out_shape=jax.ShapeDtypeStruct((LOCAL, 8, GQ, HEAD), bf),
        in_specs=[pl.BlockSpec(memory_space=pltpu.VMEM)] * 4,
        out_specs=pl.BlockSpec(memory_space=pl.ANY),
        scratch_shapes=[
            pltpu.VMEM((64, 2, BLOCK, HEAD), bf),
            pltpu.VMEM((2, 4, LOCAL * GQ, HEAD), bf),
            pltpu.VMEM((2, 4, 2, LOCAL, HEAD), bf),
            pltpu.VMEM((2, 4, 2, LOCAL, HEAD), bf),
            pltpu.VMEM((4, 2, LOCAL, HEAD), bf),
            pltpu.VMEM((4, 2, LOCAL, HEAD), bf),
            pltpu.VMEM((2, 4, LOCAL, GQ, HEAD), bf),
            pltpu.VMEM((ROWS, 4608), f32),
            pltpu.VMEM((ROWS, 4608), f32),
            pltpu.VMEM((ROWS, 128), f32),
            pltpu.VMEM((ROWS, 128), f32),
            dma((128,)), dma((64, 2)), dma((2, 4)), dma((4,)), dma((4,)), dma((4,)), dma((4,)),
            dma((2,)), dma((2, 4)), dma((8,)), dma((8,)),
        ],
        compiler_params=pltpu.CompilerParams(
            collective_id=0, has_side_effects=True, vmem_limit_bytes=60 * 2**20),
    )(q_in, sk_in, sv_in, kv_in)


def solution(mesh):
    return jax.shard_map(
        shards,
        mesh=mesh,
        in_specs=(
            P(("outer", "inner"), None, None, None),
            P("outer", "inner", None),
            P("inner", None, None),
            P("outer", "inner", None),
            P("outer", "inner"),
            P("outer"),
        ),
        out_specs=P(("outer", "inner"), None, None, None),
        check_vma=False,
    )
```

time: 321 us -> 80.2 us (0.25)
  the two profiles are of different devices: /device:TPU:32 before, /device:TPU:1 now
where the time goes in v1:
time: 80.2 us; the launch traced here: 80 us
  Pallas kernels  69.5 us (87%)
  local copies, waits for them, and re-layouts  5.33 us (7%)
  other arithmetic  3.86 us (5%)
  between operations  0.83 us (1%)
    pallas_call x1, Pallas kernels, shards(): pl.pallas_call(kernel, out_shape=jax.ShapeDtypeStruct((LOCAL, 8, GQ, HEAD...  69.5 us
    unnamed x12, local copies, waits for them, and re-layouts  2.58 us
    transpose x1, local copies, waits for them, and re-layouts, shards(): q_in = rotated[:, :, :GQ].transpose(1, 0, 2, 3).reshape(8, LOCAL * GQ, HEAD)  1.7 us

profile of v1, /device:TPU:1, one launch (start us, length us, event | category | flops | bytes accessed | tf_op | source)
XLA Modules:
  0.0 80.0 jit_solution(1363003968851930231)
XLA Ops:
  0.0 0.0 slice-start
  0.0 0.2 multiply_cosine_fusion.1
  0.2 1.0 %slice-done = bf16[64,8,9,128]{3,1,2,0:T(8,128)(2,1)S(1)} async-done(((bf16[64,8,10,128]{3,1,2,0:T(8,128)(2,1)}), bf16[64,8,9,128]{3,1,2,0:T(8,128)(2,1)S(1)}, s32[]{:S(2)}) %slice-start) | async-done | bytes 1179672 | tf_op jit(solution)/shard_map/slice | solution.py:286
  1.3 0.3 copy_convert_fusion
  1.6 0.0 slice-start.1
  1.6 0.9 %add_convert_fusion = (bf16[64,8,9,64]{3,0,1,2:T(8,128)(2,1)S(1)}, bf16[64,8,9,64]{3,0,1,2:T(8,128)(2,1)S(1)}) fusion(f32[64,8,9,128]{3,0,1,2:T(8,128)S(1)} %copy_convert_fusion, f32[64,64]{1,0:T(8,128)S(1)} %get-tuple-element.12, f32[64,64]{1,0:T(8,128)S(1)} %get-tuple-element.11), kind=kLoop, calls=%fused_computation | loop fusion | flops 2359296 | bytes 3571712 | tf_op jit(solution)/shard_map/convert.5
  2.5 0.0 slice-done.1
  2.5 0.8 fusion.9
  3.3 0.0 copy-start
  3.3 0.0 copy-start.2
  3.3 0.6 fusion.6
  3.8 0.0 copy-start.1
  3.9 0.0 copy-start.3
  3.9 1.7 %copy.24 = bf16[8,64,8,128]{3,2,1,0:T(8,128)(2,1)} copy(bf16[8,64,8,128]{3,1,0,2:T(8,128)(2,1)S(1)} %fusion.6) | data formatting | bytes 2097152 | tf_op jit(solution)/shard_map/transpose | solution.py:287
  5.6 0.0 copy-done
  5.6 0.1 copy.14
  5.7 0.0 copy-done.2
  5.7 0.5 fusion.2
  6.2 0.1 copy.19
  6.3 0.1 copy.20
  7.1 0.3 fusion.21
  7.4 0.0 copy-done.1
  7.4 0.0 copy-done.3
  7.4 0.1 fusion.19
  7.5 0.7 pad_maximum_fusion.1.kv_in
  8.2 69.5 %shard_map.64 = bf16[64,8,8,128]{3,2,1,0:T(8,128)(2,1)} custom-call(bf16[8,512,128]{2,1,0:T(8,128)(2,1)} %bitcast.34, bf16[8,64,128]{2,1,0:T(8,128)(2,1)} %get-tuple-element.13.sk_in, bf16[8,64,128]{2,1,0:T(8,128)(2,1)} %get-tuple-element.14.sv_in, bf16[2,128,128]{2,1,0:T(8,128)(2,1)} %pad_maximum_fusion.1.kv_in), custom_call_target="tpu_custom_call" | custom-call | tf_op jit(solution)/shard_map/pallas_call | solution.py:293
  77.8 2.3 %copy.27 = bf16[64,8,8,128]{3,2,1,0:T(8,128)(2,1)} copy(bf16[64,8,8,128]{3,2,1,0:T(8,128)(2,1)} %shard_map.64) | data formatting | bytes 2097152
  (6 shorter events, 0.0 us)
Async XLA Ops:
  0.0 1.3 %slice-start = ((bf16[64,8,10,128]{3,1,2,0:T(8,128)(2,1)}), bf16[64,8,9,128]{3,1,2,0:T(8,128)(2,1)S(1)}, s32[]{:S(2)}) async-start(bf16[64,8,10,128]{3,1,2,0:T(8,128)(2,1)} %param.6), calls=%async_computation | async-start | bytes 2359296 | tf_op jit(solution)/shard_map/slice | solution.py:286
  1.6 0.9 %slice-start.1 = ((bf16[64,8,10,128]{3,1,2,0:T(8,128)(2,1)}), bf16[64,8,1,128]{3,1,2,0:T(8,128)(2,1)S(1)}, s32[]{:S(2)}) async-start(bf16[64,8,10,128]{3,1,2,0:T(8,128)(2,1)} %param.6), calls=%async_computation.1 | async-start | bytes 262144 | tf_op jit(solution)/shard_map/slice | solution.py:289
  3.3 2.3 %copy-start = (bf16[1,256,128]{2,1,0:T(8,128)(2,1)S(1)}, bf16[1,256,128]{2,1,0:T(8,128)(2,1)}, u32[]{:S(2)}) copy-start(bf16[1,256,128]{2,1,0:T(8,128)(2,1)} %param.8) | copy-start | bytes 196612
  3.3 2.4 %copy-start.2 = (s32[128,1,16]{0,2,1:T(8,128)S(1)}, s32[128,1,16]{0,2,1:T(8,128)}, u32[]{:S(2)}) copy-start(s32[128,1,16]{0,2,1:T(8,128)} %param.7) | copy-start | bytes 24580
  3.8 3.6 %copy-start.1 = (bf16[128,1,128]{2,0,1:T(8,128)(2,1)S(1)}, bf16[128,1,128]{2,0,1:T(8,128)(2,1)}, u32[]{:S(2)}) copy-start(bf16[128,1,128]{2,0,1:T(8,128)(2,1)} %param.9) | copy-start | bytes 98308
  3.9 3.6 %copy-start.3 = (f32[128,1]{0,1:T(1,128)S(1)}, f32[128,1]{0,1:T(1,128)}, u32[]{:S(2)}) copy-start(f32[128,1]{0,1:T(1,128)} %param.10) | copy-start | bytes 1540

commit v2 on v1

--- a/solution.py
+++ b/solution.py
@@ -70,14 +70,18 @@
         pl.semaphore_signal(barrier, inc=1, device_id=peer, device_id_type=pl.DeviceIdType.MESH)
     pl.semaphore_wait(barrier, len(peers))
 
-    sent = []
+    sent, ends = [], []
+    likes = {r.shape: r for r in (kv.at[0], kv.at[0, 0], rk.at[0], rk, qb.at[0, 0])}
 
     def put(src, dst, recv_sem, to):
         copy = pltpu.make_async_remote_copy(
             src_ref=src, dst_ref=dst, send_sem=send.at[len(sent)], recv_sem=recv_sem,
             device_id=to, device_id_type=pl.DeviceIdType.MESH)
         copy.start()
-        sent.append(copy)
+        index = len(sent)
+        sent.append(index)
+        like = likes[src.shape]
+        ends.append(lambda: pltpu.make_async_copy(like, like, send.at[index]).wait())
 
     def got(dst, recv_sem):
         pltpu.make_async_copy(dst, dst, recv_sem).wait()
@@ -105,7 +109,7 @@
             put(sk_in.at[pair], sk.at[zh, y], rsk.at[y], dev(dy=d))
             put(sv_in.at[pair], sv.at[zh, y], rsv.at[y], dev(dy=d))
     for hh in (zh, 1 - zh):
-        for d in range(4):
+        for d in (0, 3, 1, 2):
             yd = (y + d) % NY
             if d == 0:
                 keep(q_in.at[2 * yd + hh], qb.at[hh, y])
@@ -117,7 +121,21 @@
         put(kv.at[s], kv.at[s], rs.at[s, 0], dev(dx=-1))
         put(kv.at[s], kv.at[s], rs.at[s, 0], dev(dc=1))
 
-    for d in (1, 2, 3):
+    def relay(dz):
+        for sign in (-1, 1):
+            s = slot(dz, sign)
+            got(kv.at[s], rs.at[s, 0])
+            half = 0 if sign < 0 else 1
+            put(kv.at[s, half], kv.at[s, half], rs.at[s, half], dev(dx=-sign))
+            put(kv.at[s], kv.at[s], rs.at[s, 0], dev(dc=1))
+
+    def close(dz):
+        s = slot(dz, 2)
+        got(kv.at[s, 0], rs.at[s, 0])
+        got(kv.at[s, 1], rs.at[s, 1])
+        put(kv.at[s], kv.at[s], rs.at[s, 0], dev(dc=1))
+
+    def ring(d):
         for sign in (-1, 1):
             s = slot(sign * d, 0)
             got(kv.at[s], rs.at[s, 0])
@@ -126,48 +144,57 @@
             else:
                 half = 0 if sign < 0 else 1
                 put(kv.at[s, half], kv.at[s, half], rs.at[s, half], dev(dz=-sign))
-            spread(s)
-    s = slot(4, 0)
-    got(kv.at[s, 0], rs.at[s, 0])
-    got(kv.at[s, 1], rs.at[s, 1])
-    spread(s)
-
+
+    first, last = (zl == 0).astype(jnp.int32), (zl == 3).astype(jnp.int32)
+    third = (zl == 2).astype(jnp.int32)
+    near = [0, 1 - 2 * last, 1 + first - 3 * last, 2 + first - 4 * third - 5 * last]
+    near[1] = 1 - 2 * last
+    near[2] = first * 2 + last * -2 + (1 - first - last) * -1
+    near[3] = first * 3 + last * -3 + third * -2 + (1 - first - last - third) * 2
+
+    def far(k):
+        return (zh * 4 + 4 + k) - z
+
+    ring(1)
+    spread(slot(near[1], 0))
+    relay(0)
+    ring(2)
+    spread(slot(near[2], 0))
+    ring(3)
+    spread(slot(near[3], 0))
+    relay(near[1])
     for src in range(NY):
         got(rk.at[src], rrk.at[src])
         got(rv.at[src], rrv.at[src])
     put(rk, sk.at[((z + 6) % NZ) // NH], rx.at[0], dev(dz=2))
     put(rv, sv.at[((z + 2) % NZ) // NH], rx.at[1], dev(dz=-2))
-
-    order = (0, -1, 1, -2, 2, -3, 3, 4)
-    for dz in order:
-        for sign in (-1, 1):
-            s = slot(dz, sign)
-            got(kv.at[s], rs.at[s, 0])
-            half = 0 if sign < 0 else 1
-            put(kv.at[s, half], kv.at[s, half], rs.at[s, half], dev(dx=-sign))
-            put(kv.at[s], kv.at[s], rs.at[s, 0], dev(dc=1))
-    for dz in order:
-        s = slot(dz, 2)
-        got(kv.at[s, 0], rs.at[s, 0])
-        got(kv.at[s, 1], rs.at[s, 1])
-        put(kv.at[s], kv.at[s], rs.at[s, 0], dev(dc=1))
-    for dz in order:
-        for dx in range(4):
-            s = slot(dz, dx, 1)
-            got(kv.at[s], rs.at[s, 0])
-    for d in (1, 2, 3):
-        src = (y + d) % NY
-        got(sk.at[zh, src], rsk.at[src])
-        got(sv.at[zh, src], rsv.at[src])
-        for hh in range(2):
-            got(qb.at[hh, src], rq.at[hh, src])
-    got(sk.at[1 - zh], rx.at[0])
-    got(sv.at[1 - zh], rx.at[1])
+    relay(near[2])
+    relay(near[3])
+    s = slot(4, 0)
+    got(kv.at[s, 0], rs.at[s, 0])
+    got(kv.at[s, 1], rs.at[s, 1])
+    for k in range(4):
+        spread(slot(far(k), 0))
+    for k in range(4):
+        close(near[k])
     for copy in kept:
         copy.wait()
+    for k in range(4):
+        for dx in range(4):
+            s = slot(near[k], dx, 1)
+            got(kv.at[s], rs.at[s, 0])
+
+    def stretch_ready():
+        for d in (1, 2, 3):
+            src = (y + d) % NY
+            got(sk.at[zh, src], rsk.at[src])
+            got(sv.at[zh, src], rsv.at[src])
+        got(sk.at[1 - zh], rx.at[0])
+        got(sv.at[1 - zh], rx.at[1])
 
     def unit(u):
-        return (zh + u // 4) % 2, (y + 1 + u % 4) % NY
+        k = min(u, 7 - u) if isinstance(u, int) else jnp.minimum(u, 7 - u)
+        return (zh + u // 4) % 2, (y + k * (k + 1) // 2) % NY
 
     def keys_of(hh, n):
         if n < 8:
@@ -219,6 +246,8 @@
     def stage(tn, bufn, mn, tc, bufc, mc):
         top, total = None, None
         for n in range(len(spans)):
+            if tc is None and n == 8:
+                stretch_ready()
             if tn is not None:
                 part = score(tn, n, bufn)
                 top = part if top is None else jnp.maximum(top, part)
@@ -248,24 +277,52 @@
 
     def body(u, carry):
         stage(2 * u + 1, sb, mb, 2 * u, sa, ma)
+
+        @pl.when((u < 6))
+        def _():
+            hh, src = unit(u + 1)
+            got(qb.at[hh, src], rq.at[hh, src])
+
+        @pl.when(u == 3)
+        def _():
+            for k in range(4):
+                for dx in range(4):
+                    s = slot(far(k), dx, 1)
+                    got(kv.at[s], rs.at[s, 0])
+
         stage(jnp.minimum(2 * u + 2, 15), sa, ma, 2 * u + 1, sb, mb)
 
-        @pl.when(u % 4 < 3)
+        @pl.when((u > 0) & (u < 7))
         def _():
             result_copy(u).start()
 
-        @pl.when(u % 4 == 3)
+        @pl.when((u == 0) | (u == 7))
         def _():
             own_copy(u).start()
 
+        @pl.when(u == 0)
+        def _():
+            relay(far(0))
+            relay(far(1))
+
+        @pl.when(u == 1)
+        def _():
+            relay(far(2))
+            relay(far(3))
+
+        @pl.when(u == 2)
+        def _():
+            for k in range(4):
+                close(far(k))
+
         return carry
 
     lax.fori_loop(0, 8, body, 0)
 
-    for copy in sent:
-        copy.wait_send()
+    for wait in ends:
+        wait()
     for u in range(8):
-        if u % 4 == 3:
+        if u in (0, 7):
             own_copy(u).wait()
         else:
             result_copy(u).wait_send()

time: 80.2 us -> 78.3 us (0.976)
  Pallas kernels: 69.5 us -> 67.6 us
    pallas_call x1, Pallas kernels: 69.5 us -> 67.6 us  [shards(): pl.pallas_call(kernel, out_shape=jax.ShapeDtypeStruct((LOCAL, 8, GQ, HEAD...]
where the time goes in v2:
time: 78.3 us; the launch traced here: 78.1 us
  Pallas kernels  67.6 us (86%)
  local copies, waits for them, and re-layouts  5.33 us (7%)
  other arithmetic  3.86 us (5%)
  between operations  0.83 us (1%)
    pallas_call x1, Pallas kernels, shards(): pl.pallas_call(kernel, out_shape=jax.ShapeDtypeStruct((LOCAL, 8, GQ, HEAD...  67.6 us
    unnamed x12, local copies, waits for them, and re-layouts  2.58 us
    transpose x1, local copies, waits for them, and re-layouts, shards(): q_in = rotated[:, :, :GQ].transpose(1, 0, 2, 3).reshape(8, LOCAL * GQ, HEAD)  1.7 us

profile of v2, /device:TPU:1, one launch (start us, length us, event | category | flops | bytes accessed | tf_op | source)
XLA Modules:
  0.0 78.1 jit_solution(4829995782009120461)
XLA Ops:
  0.0 0.0 slice-start
  0.0 0.2 multiply_cosine_fusion.1
  0.2 1.0 %slice-done = bf16[64,8,9,128]{3,1,2,0:T(8,128)(2,1)S(1)} async-done(((bf16[64,8,10,128]{3,1,2,0:T(8,128)(2,1)}), bf16[64,8,9,128]{3,1,2,0:T(8,128)(2,1)S(1)}, s32[]{:S(2)}) %slice-start) | async-done | bytes 1179672 | tf_op jit(solution)/shard_map/slice | solution.py:343
  1.3 0.3 copy_convert_fusion
  1.6 0.0 slice-start.1
  1.6 0.9 %add_convert_fusion = (bf16[64,8,9,64]{3,0,1,2:T(8,128)(2,1)S(1)}, bf16[64,8,9,64]{3,0,1,2:T(8,128)(2,1)S(1)}) fusion(f32[64,8,9,128]{3,0,1,2:T(8,128)S(1)} %copy_convert_fusion, f32[64,64]{1,0:T(8,128)S(1)} %get-tuple-element.12, f32[64,64]{1,0:T(8,128)S(1)} %get-tuple-element.11), kind=kLoop, calls=%fused_computation | loop fusion | flops 2359296 | bytes 3571712 | tf_op jit(solution)/shard_map/convert.5
  2.5 0.0 slice-done.1
  2.5 0.8 fusion.9
  3.3 0.0 copy-start
  3.3 0.0 copy-start.2
  3.3 0.6 fusion.6
  3.8 0.0 copy-start.1
  3.9 0.0 copy-start.3
  3.9 1.7 %copy.24 = bf16[8,64,8,128]{3,2,1,0:T(8,128)(2,1)} copy(bf16[8,64,8,128]{3,1,0,2:T(8,128)(2,1)S(1)} %fusion.6) | data formatting | bytes 2097152 | tf_op jit(solution)/shard_map/transpose | solution.py:344
  5.6 0.0 copy-done
  5.6 0.1 copy.14
  5.7 0.0 copy-done.2
  5.7 0.5 fusion.2
  6.2 0.1 copy.19
  6.3 0.1 copy.20
  7.1 0.3 fusion.21
  7.4 0.0 copy-done.1
  7.4 0.0 copy-done.3
  7.4 0.1 fusion.19
  7.5 0.7 pad_maximum_fusion.1.kv_in
  8.2 67.6 %shard_map.64 = bf16[64,8,8,128]{3,2,1,0:T(8,128)(2,1)} custom-call(bf16[8,512,128]{2,1,0:T(8,128)(2,1)} %bitcast.34, bf16[8,64,128]{2,1,0:T(8,128)(2,1)} %get-tuple-element.13.sk_in, bf16[8,64,128]{2,1,0:T(8,128)(2,1)} %get-tuple-element.14.sv_in, bf16[2,128,128]{2,1,0:T(8,128)(2,1)} %pad_maximum_fusion.1.kv_in), custom_call_target="tpu_custom_call" | custom-call | tf_op jit(solution)/shard_map/pallas_call | solution.py:350
  75.8 2.3 %copy.27 = bf16[64,8,8,128]{3,2,1,0:T(8,128)(2,1)} copy(bf16[64,8,8,128]{3,2,1,0:T(8,128)(2,1)} %shard_map.64) | data formatting | bytes 2097152
  (6 shorter events, 0.0 us)
Async XLA Ops:
  0.0 1.3 %slice-start = ((bf16[64,8,10,128]{3,1,2,0:T(8,128)(2,1)}), bf16[64,8,9,128]{3,1,2,0:T(8,128)(2,1)S(1)}, s32[]{:S(2)}) async-start(bf16[64,8,10,128]{3,1,2,0:T(8,128)(2,1)} %param.6), calls=%async_computation | async-start | bytes 2359296 | tf_op jit(solution)/shard_map/slice | solution.py:343
  1.6 0.9 %slice-start.1 = ((bf16[64,8,10,128]{3,1,2,0:T(8,128)(2,1)}), bf16[64,8,1,128]{3,1,2,0:T(8,128)(2,1)S(1)}, s32[]{:S(2)}) async-start(bf16[64,8,10,128]{3,1,2,0:T(8,128)(2,1)} %param.6), calls=%async_computation.1 | async-start | bytes 262144 | tf_op jit(solution)/shard_map/slice | solution.py:346
  3.3 2.3 %copy-start = (bf16[1,256,128]{2,1,0:T(8,128)(2,1)S(1)}, bf16[1,256,128]{2,1,0:T(8,128)(2,1)}, u32[]{:S(2)}) copy-start(bf16[1,256,128]{2,1,0:T(8,128)(2,1)} %param.8) | copy-start | bytes 196612
  3.3 2.4 %copy-start.2 = (s32[128,1,16]{0,2,1:T(8,128)S(1)}, s32[128,1,16]{0,2,1:T(8,128)}, u32[]{:S(2)}) copy-start(s32[128,1,16]{0,2,1:T(8,128)} %param.7) | copy-start | bytes 24580
  3.8 3.6 %copy-start.1 = (bf16[128,1,128]{2,0,1:T(8,128)(2,1)S(1)}, bf16[128,1,128]{2,0,1:T(8,128)(2,1)}, u32[]{:S(2)}) copy-start(bf16[128,1,128]{2,0,1:T(8,128)(2,1)} %param.9) | copy-start | bytes 98308
  3.9 3.6 %copy-start.3 = (f32[128,1]{0,1:T(1,128)S(1)}, f32[128,1]{0,1:T(1,128)}, u32[]{:S(2)}) copy-start(f32[128,1]{0,1:T(1,128)} %param.10) | copy-start | bytes 1540

commit v3 on v0

v3 whole, which is shorter than its diff:
```python
import functools
import math

import jax
import jax.numpy as jnp
import numpy as np
from jax import lax
from jax.experimental import pallas as pl
from jax.experimental.pallas import tpu as pltpu
from jax.sharding import PartitionSpec as P

rope_base = 500000.0
NX, NY, NZ, NH = 4, 4, 8, 4
BLOCK, HEAD, GQ, LOCAL, CODES, GROUPS, PREFIX = 128, 128, 8, 64, 256, 16, 4096
ROWS = 256
SCALE = 128**-0.5 * math.log2(math.e)
NT = (((1,), (1,)), ((), ()))
SPANS = [(512 * n, 512) for n in range(8)] + [(4096, 256), (4352, 256)]
WIDTH = 4608


def rope_tables():
    step = np.float32(-2.0 * math.log(rope_base) / HEAD)
    inverse = np.exp((np.arange(64, dtype=np.float32) * step).astype(np.float64)).astype(np.float32).astype(np.float64)
    inverse = np.concatenate([inverse, inverse])
    fine = np.arange(BLOCK)[:, None] * inverse
    starts = np.concatenate([np.arange(32) * BLOCK, PREFIX + np.arange(8) * LOCAL])
    coarse = starts[:, None] * inverse
    table = np.concatenate([np.cos(fine), np.sin(fine), np.cos(coarse), np.sin(coarse)])
    return jnp.asarray(table.astype(np.float32))


def kernel(qkv, codes, books, vcodes, scales, block, table, out,
           kv, qs, sks, svs, qb, sk, sv, ob, xs, cq, sq, g0, g1, mx,
           send, rs, rq, rsk, rsv, ro, loc, osend):
    o = lax.axis_index("outer")
    i = lax.axis_index("inner")
    zl, x, c = o // 8, (o // 2) % NX, o % 2
    y, zh = i // 2, i % 2

    def dev(dx=0, dy=0, dz=0, far=0, dc=0):
        outer = ((zl + dz) % NH) * 8 + ((x + dx) % NX) * 2 + (c + dc) % 2
        return {"outer": outer, "inner": ((y + dy) % NY) * 2 + (zh + far) % 2}

    peers = [dev(dz=d) for d in (1, 2, 3)] + [dev(dz=d, far=1) for d in range(4)]
    peers += [dev(dx=1), dev(dx=3), dev(dc=1)]
    peers += [dev(dy=d) for d in (1, 2, 3)] + [dev(dy=d, far=1) for d in (1, 2, 3)]
    barrier = pltpu.get_barrier_semaphore()
    for peer in peers:
        pl.semaphore_signal(barrier, inc=1, device_id=peer, device_id_type=pl.DeviceIdType.MESH)

    def slot(half, side, core, k):
        return ((half * 4 + side) * 2 + core) * 4 + k

    def angles(start, rows):
        fine_c, fine_s = table[:rows], table[BLOCK:BLOCK + rows]
        base_c = table[pl.ds(2 * BLOCK + start, 1), :]
        base_s = table[pl.ds(2 * BLOCK + 40 + start, 1), :]
        lane = lax.broadcasted_iota(jnp.int32, (rows, HEAD), 1)
        sine = base_s * fine_c + base_c * fine_s
        return base_c * fine_c - base_s * fine_s, jnp.where(lane < HEAD // 2, -sine, sine)

    book_t = books[...].astype(jnp.float32).T
    entry = lax.broadcasted_iota(jnp.int32, (CODES, BLOCK), 0)
    parts = []
    for g in range(GROUPS):
        hot = jnp.where(entry == codes[g:g + 1, :], 1.0, 0.0).astype(jnp.bfloat16)
        rows = book_t[8 * g:8 * g + 8, :].astype(jnp.bfloat16)
        parts.append(jnp.dot(rows, hot, preferred_element_type=jnp.float32))
    keys = jnp.concatenate(parts, axis=0).T
    cosine, sine = angles(block[0], BLOCK)
    own = slot(0, 0, 0, 0)
    kv[own, 0] = (keys * cosine + pltpu.roll(keys, HEAD // 2, 1) * sine).astype(jnp.bfloat16)
    scale = jnp.broadcast_to(scales[...], (BLOCK, BLOCK)).T
    kv[own, 1] = (vcodes[...].astype(jnp.float32) * scale).astype(jnp.bfloat16)
    cq[...], sq[...] = angles(32 + i, LOCAL)

    pl.semaphore_wait(barrier, len(peers))

    sent, ends = [], []
    likes = {r.shape: r for r in (kv.at[0], kv.at[0, 0], sks.at[pl.ds(0, 2)], qb.at[0, 0])}

    def put(src, dst, recv_sem, to):
        index = len(sent)
        sent.append(index)
        pltpu.make_async_remote_copy(
            src_ref=src, dst_ref=dst, send_sem=send.at[index], recv_sem=recv_sem,
            device_id=to, device_id_type=pl.DeviceIdType.MESH).start()
        like = likes[src.shape]
        ends.append(lambda: pltpu.make_async_copy(like, like, send.at[index]).wait())

    def got(dst, recv_sem):
        pltpu.make_async_copy(dst, dst, recv_sem).wait()

    kept = []

    def keep(src, dst):
        copy = pltpu.make_async_copy(src, dst, loc.at[len(kept)])
        copy.start()
        kept.append(copy)

    def full(half, side, core, k):
        s = slot(half, side, core, k)
        got(kv.at[s], rs.at[s, 0])

    def to_sides(half, k):
        src = kv.at[slot(half, 0, 0, k)]
        for side, dx in ((1, 1), (2, 3)):
            s = slot(half, side, 0, k)
            put(src, kv.at[s], rs.at[s, 0], dev(dx=dx))

    def to_core(half, side, k):
        s = slot(half, side, 1, k)
        put(kv.at[slot(half, side, 0, k)], kv.at[s], rs.at[s, 0], dev(dc=1))

    def relay(half, k):
        for side, dx in ((1, 1), (2, 3)):
            full(half, side, 0, k)
            s = slot(half, 3, 0, k)
            part = side - 1
            put(kv.at[slot(half, side, 0, k), part], kv.at[s, part], rs.at[s, part], dev(dx=dx))
            to_core(half, side, k)

    def close(half, k):
        s = slot(half, 3, 0, k)
        got(kv.at[s, 0], rs.at[s, 0])
        got(kv.at[s, 1], rs.at[s, 1])
        to_core(half, 3, k)

    to_sides(0, 0)
    for d in (1, 3, 2):
        s = slot(0, 0, 0, 4 - d)
        put(kv.at[own], kv.at[s], rs.at[s, 0], dev(dz=d))
    to_core(0, 0, 0)

    def turn(t, carry):
        rows = qkv[t].astype(jnp.float32)
        cosine, sine = cq[pl.ds(t, 1), :], sq[pl.ds(t, 1), :]
        head = rows[:9].reshape(72, HEAD)
        xs[pl.ds(pl.multiple_of(t * 80, 8), 72), :] = head * cosine + pltpu.roll(head, HEAD // 2, 1) * sine
        xs[pl.ds(pl.multiple_of(t * 80 + 72, 8), 8), :] = rows[9]
        return carry

    lax.fori_loop(0, LOCAL, turn, 0, unroll=4)
    for h in range(8):
        sks[h] = xs[pl.ds(64 + h, LOCAL, stride=80), :].astype(jnp.bfloat16)
        svs[h] = xs[pl.ds(72 + h, LOCAL, stride=80), :].astype(jnp.bfloat16)
    for d in range(4):
        pair = pl.ds(2 * ((y + d) % NY), 2)
        back = (4 - d) % 4
        put(sks.at[pair], sk.at[1, y], rsk.at[1, back], dev(dy=d, far=1))
        put(svs.at[pair], sv.at[1, y], rsv.at[1, back], dev(dy=d, far=1))
        if d == 0:
            keep(sks.at[pair], sk.at[0, y])
            keep(svs.at[pair], sv.at[0, y])
        else:
            put(sks.at[pair], sk.at[0, y], rsk.at[0, back], dev(dy=d))
            put(svs.at[pair], sv.at[0, y], rsv.at[0, back], dev(dy=d))

    def gather(t, carry):
        for h in range(8):
            two = [xs[pl.ds(t * 160 + 80 * j + h, 8, stride=8), :] for j in range(2)]
            qs[h, pl.ds(pl.multiple_of(t * 16, 16), 16), :] = jnp.concatenate(two, axis=0).astype(jnp.bfloat16)
        return carry

    lax.fori_loop(0, LOCAL // 2, gather, 0, unroll=2)
    for hr in range(2):
        for d in (0, 3, 1, 2):
            src = qs.at[2 * ((y + d) % NY) + (zh + hr) % 2]
            back = (4 - d) % 4
            if d == 0:
                keep(src, qb.at[hr, 0])
            else:
                put(src, qb.at[hr, back], rq.at[hr, back], dev(dy=d))
    for d in (0, 1, 3, 2):
        s = slot(1, 0, 0, (4 - d) % 4)
        put(kv.at[own], kv.at[s], rs.at[s, 0], dev(dz=d, far=1))

    def unit(u):
        k = min(u, 7 - u) if isinstance(u, int) else jnp.minimum(u, 7 - u)
        return u // 4, (k * (k + 1) // 2) % 4

    def token_block(hr, n, part):
        if n < 8:
            return kv[pl.ds(hr * 32 + 4 * n, 4), part].reshape(4 * BLOCK, HEAD)
        ref = sk if part == 0 else sv
        return ref[n - 8, :, (zh + hr) % 2].reshape(4 * LOCAL, HEAD)

    def query_tile(t):
        hr, d = unit(t // 2)
        floats = qb[hr, d, pl.ds(pl.multiple_of((t % 2) * ROWS, ROWS), ROWS), :].astype(jnp.float32) * SCALE
        high = floats.astype(jnp.bfloat16)
        low = (floats - high.astype(jnp.float32)).astype(jnp.bfloat16)
        return jnp.concatenate([high, low], axis=1)

    def score(t, n, buf, j):
        hr, d = unit(t // 2)
        keys = token_block(hr, n, 0)
        first, size = SPANS[n]
        keys = jnp.concatenate([keys, keys], axis=1)
        s = lax.dot_general(query_tile(t), keys, NT, preferred_element_type=jnp.float32)
        if n >= 8:
            token = (2 * ((y + d) % NY) + zh) * LOCAL + (t % 2) * (ROWS // GQ)
            row = token + lax.broadcasted_iota(jnp.int32, (ROWS, size), 0) // GQ
            col = lax.broadcasted_iota(jnp.int32, (ROWS, size), 1)
            col = (col // LOCAL) * (2 * LOCAL) + ((zh + n) % 2) * LOCAL + col % LOCAL
            s = jnp.where(col <= row, s, -1e30)
        buf[j, :, first:first + size] = s
        top = s[:, :128]
        for m in range(1, size // 128):
            top = jnp.maximum(top, s[:, m * 128:(m + 1) * 128])
        return top

    def weigh(t, n, buf, j, top):
        hr, _ = unit(t // 2)
        first, size = SPANS[n]
        weights = jnp.exp2(buf[j, :, first:first + size] - top).astype(jnp.bfloat16)
        values = token_block(hr, n, 1)
        values = jnp.concatenate([values, jnp.ones_like(values)], axis=1)
        return jnp.dot(weights, values, preferred_element_type=jnp.float32)

    def widest(top):
        return jnp.broadcast_to(jnp.max(top, axis=1, keepdims=True), (ROWS, 128))

    def stage(t, buf, j, tn=None, bufn=None):
        top, total = None, None
        peak = mx[t % 8][:, :1]
        for n in range(len(SPANS)):
            if tn is not None:
                part = score(tn, n, bufn, j)
                top = part if top is None else jnp.maximum(top, part)
            part = weigh(t, n, buf, j, peak)
            total = part if total is None else total + part
        if tn is not None:
            mx[tn % 8] = widest(top)
        hr, d = unit(t // 2)
        result = (total[:, :HEAD] / total[:, HEAD:]).reshape(ROWS // GQ, GQ, HEAD)
        at = pl.ds(pl.multiple_of((t % 2) * (ROWS // GQ), ROWS // GQ), ROWS // GQ)
        ob[hr, d, at] = result.astype(jnp.bfloat16)

    def head_of(hr):
        return 2 * y + (zh + hr) % 2

    def result_copy(u):
        hr, d = unit(u)
        return pltpu.make_async_remote_copy(
            src_ref=ob.at[hr, d], dst_ref=out.at[:, head_of(hr)],
            send_sem=osend.at[u], recv_sem=ro.at[hr, (4 - d) % 4],
            device_id=dev(dy=d), device_id_type=pl.DeviceIdType.MESH)

    def own_copy(u):
        hr, d = unit(u)
        return pltpu.make_async_copy(ob.at[hr, d], out.at[:, head_of(hr)], osend.at[u])

    def deliver(t):
        @pl.when((t % 2 == 1) & (t != 1) & (t != 15))
        def _():
            result_copy(t // 2).start()

        @pl.when((t == 1) | (t == 15))
        def _():
            own_copy(t // 2).start()

    def early(n, first=False):
        def two(j, carry):
            for half, buf in ((0, g0), (1, g1)):
                t = 4 * half + j
                part = score(t, n, buf, j)
                mx[t] = part if first else jnp.maximum(mx[t], part)
            return carry
        lax.fori_loop(0, 4, two, 0)

    first = (zl == 0).astype(jnp.int32)
    last = (zl == NH - 1).astype(jnp.int32)
    ka = 1 + 2 * last
    kb = 3 - first - last
    near = (0, ka, kb, 6 - ka - kb)
    for n in (1, 2, 3):
        full(0, 0, 0, near[n])
        to_sides(0, near[n])
        to_core(0, 0, near[n])
        relay(0, near[n - 1])
    for copy in kept:
        copy.wait()
    for d in (1, 3, 2):
        got(qb.at[0, d], rq.at[0, d])
    early(0, True)
    relay(0, near[3])
    for n in range(4):
        full(0, 0, 1, n)
    early(1)
    for n in range(4):
        close(0, near[n])
    early(2)
    early(4)
    for n in range(4):
        full(1, 0, 0, n)
        to_sides(1, n)
        to_core(1, 0, n)
    for n in range(4):
        full(0, 1, 1, n)
        full(0, 2, 1, n)
    early(3)
    early(5)
    early(6)
    for n in range(4):
        full(0, 3, 1, n)
    early(7)
    for d in range(4):
        for zr in range(2):
            if d > 0 or zr > 0:
                src = (y + d) % NY
                got(sk.at[zr, src], rsk.at[zr, d])
                got(sv.at[zr, src], rsv.at[zr, d])
    early(8)
    early(9)
    for t in range(8):
        mx[t] = widest(mx[t])

    def loop(start, step):
        def body(j, carry):
            step(j)
            deliver(start + j)
            return carry
        lax.fori_loop(0, 4, body, 0)

    def opening(j):
        stage(j, g0, j)

        @pl.when(j == 0)
        def _():
            relay(1, 0)
            relay(1, 1)

        @pl.when(j == 1)
        def _():
            relay(1, 2)
            relay(1, 3)

        @pl.when(j == 3)
        def _():
            for n in range(4):
                close(1, n)

    loop(0, opening)
    for side in range(4):
        for n in range(4):
            full(1, side, 1, n)
    for d in (1, 3, 2):
        got(qb.at[1, d], rq.at[1, d])
    loop(4, lambda j: stage(4 + j, g1, j, 8 + j, g0))
    loop(8, lambda j: stage(8 + j, g0, j, 12 + j, g1))
    loop(12, lambda j: stage(12 + j, g1, j))

    for wait in ends:
        wait()
    for u in range(8):
        if u in (0, 7):
            own_copy(u).wait()
        else:
            result_copy(u).wait_send()
    for hr in range(2):
        for d in (1, 2, 3):
            got(out.at[:, 2 * ((y + d) % NY) + (zh + hr) % 2], ro.at[hr, d])


def shards(qkv, key_codes, codebooks, value_codes, value_scales, block_ids):
    bf, f32 = jnp.bfloat16, jnp.float32
    dma = pltpu.SemaphoreType.DMA
    vmem = pl.BlockSpec(memory_space=pltpu.VMEM)
    return pl.pallas_call(
        kernel,
        out_shape=jax.ShapeDtypeStruct((LOCAL, 8, GQ, HEAD), bf),
        in_specs=[vmem] * 5 + [pl.BlockSpec(memory_space=pltpu.SMEM), vmem],
        out_specs=pl.BlockSpec(memory_space=pl.ANY),
        scratch_shapes=[
            pltpu.VMEM((64, 2, BLOCK, HEAD), bf),
            pltpu.VMEM((8, LOCAL * GQ, HEAD), bf),
            pltpu.VMEM((8, LOCAL, HEAD), bf),
            pltpu.VMEM((8, LOCAL, HEAD), bf),
            pltpu.VMEM((2, 4, LOCAL * GQ, HEAD), bf),
            pltpu.VMEM((2, 4, 2, LOCAL, HEAD), bf),
            pltpu.VMEM((2, 4, 2, LOCAL, HEAD), bf),
            pltpu.VMEM((2, 4, LOCAL, GQ, HEAD), bf),
            pltpu.VMEM((LOCAL * 80, HEAD), f32),
            pltpu.VMEM((LOCAL, HEAD), f32),
            pltpu.VMEM((LOCAL, HEAD), f32),
            pltpu.VMEM((4, ROWS, WIDTH), f32),
            pltpu.VMEM((4, ROWS, WIDTH), f32),
            pltpu.VMEM((8, ROWS, 128), f32),
            dma((128,)), dma((64, 2)), dma((2, 4)), dma((2, 4)), dma((2, 4)),
            dma((2, 4)), dma((8,)), dma((8,)),
        ],
        compiler_params=pltpu.CompilerParams(
            collective_id=0, has_side_effects=True, vmem_limit_bytes=60 * 2**20),
    )(qkv.transpose(0, 2, 1, 3), key_codes[:, 0].T, codebooks[0], value_codes[:, 0],
      value_scales.T, block_ids, rope_tables())


def solution(mesh):
    return jax.shard_map(
        shards,
        mesh=mesh,
        in_specs=(
            P(("outer", "inner"), None, None, None),
            P("outer", "inner", None),
            P("inner", None, None),
            P("outer", "inner", None),
            P("outer", "inner"),
            P("outer"),
        ),
        out_specs=P(("outer", "inner"), None, None, None),
        check_vma=False,
    )
```

time: 321 us -> 87.9 us (0.27)
  the two profiles are of different devices: /device:TPU:32 before, /device:TPU:1 now
where the time goes in v3:
time: 87.9 us; the launch traced here: 87.8 us
  Pallas kernels  84.8 us (96%)
  local copies, waits for them, and re-layouts  2.26 us (3%)
    pallas_call x1, Pallas kernels, shards(): pl.pallas_call(kernel, out_shape=jax.ShapeDtypeStruct((LOCAL, 8, GQ, HEAD...  84.8 us
    unnamed x1, local copies, waits for them, and re-layouts  2.26 us

profile of v3, /device:TPU:1, one launch (start us, length us, event | category | flops | bytes accessed | tf_op | source)
XLA Modules:
  0.0 87.8 jit_solution(14051917284068569549)
XLA Ops:
  0.7 84.8 %shard_map.73 = bf16[64,8,8,128]{3,2,1,0:T(8,128)(2,1)} custom-call(bf16[64,10,8,128]{3,2,1,0:T(8,128)(2,1)} %bitcast.7, s32[16,128]{1,0:T(8,128)} %bitcast.10, bf16[256,128]{1,0:T(8,128)(2,1)} %bitcast.8, bf16[128,128]{1,0:T(8,128)(2,1)} %bitcast.9, f32[1,128]{1,0:T(1,128)} %bitcast.11, s32[1]{0:T(128)S(6)} %copy.9.block, f32[336,128]{1,0:T(8,128)} %constant.2.clone.table), custom_call_target="tpu_custom_call" | custom-call | tf_op jit(solution)/shard_map/pallas_call | solution.py:371
  85.5 2.3 %copy.10 = bf16[64,8,8,128]{3,2,1,0:T(8,128)(2,1)} copy(bf16[64,8,8,128]{3,2,1,0:T(8,128)(2,1)} %shard_map.73) | data formatting | bytes 2097152

commit v4 on v3

--- a/solution.py
+++ b/solution.py
@@ -31,26 +31,31 @@
 
 
 def kernel(qkv, codes, books, vcodes, scales, block, table, out,
-           kv, qs, sks, svs, qb, sk, sv, ob, xs, cq, sq, g0, g1, mx,
+           kv, qs, sks, svs, qb, sk, sv, rk, rv, ob, xs, cq, sq, g0, g1, mx,
            send, rs, rq, rsk, rsv, ro, loc, osend):
     o = lax.axis_index("outer")
     i = lax.axis_index("inner")
     zl, x, c = o // 8, (o // 2) % NX, o % 2
     y, zh = i // 2, i % 2
-
-    def dev(dx=0, dy=0, dz=0, far=0, dc=0):
-        outer = ((zl + dz) % NH) * 8 + ((x + dx) % NX) * 2 + (c + dc) % 2
-        return {"outer": outer, "inner": ((y + dy) % NY) * 2 + (zh + far) % 2}
-
-    peers = [dev(dz=d) for d in (1, 2, 3)] + [dev(dz=d, far=1) for d in range(4)]
-    peers += [dev(dx=1), dev(dx=3), dev(dc=1)]
-    peers += [dev(dy=d) for d in (1, 2, 3)] + [dev(dy=d, far=1) for d in (1, 2, 3)]
+    z = zh * NH + zl
+
+    def dev(dx=0, dy=0, dz=0, dc=0):
+        z1 = (z + dz) % NZ
+        outer = (z1 % NH) * 8 + ((x + dx) % NX) * 2 + (c + dc) % 2
+        return {"outer": outer, "inner": ((y + dy) % NY) * 2 + z1 // NH}
+
+    peers = [dev(dz=d) for d in (1, -1, 2, -2)] + [dev(dx=1), dev(dx=3), dev(dc=1)]
+    peers += [dev(dy=d) for d in (1, 2, 3)]
     barrier = pltpu.get_barrier_semaphore()
     for peer in peers:
         pl.semaphore_signal(barrier, inc=1, device_id=peer, device_id_type=pl.DeviceIdType.MESH)
 
     def slot(half, side, core, k):
         return ((half * 4 + side) * 2 + core) * 4 + k
+
+    def z_slot(src, at=0):
+        half = (((z + src) % NZ) // NH + ((z + at) % NZ) // NH) % 2
+        return slot(half, 0, 0, (src - at) % 4)
 
     def angles(start, rows):
         fine_c, fine_s = table[:rows], table[BLOCK:BLOCK + rows]
@@ -78,7 +83,7 @@
     pl.semaphore_wait(barrier, len(peers))
 
     sent, ends = [], []
-    likes = {r.shape: r for r in (kv.at[0], kv.at[0, 0], sks.at[pl.ds(0, 2)], qb.at[0, 0])}
+    likes = {r.shape: r for r in (kv.at[0], kv.at[0, 0], sks.at[pl.ds(0, 2)], qb.at[0, 0], rk)}
 
     def put(src, dst, recv_sem, to):
         index = len(sent)
@@ -127,10 +132,21 @@
         got(kv.at[s, 1], rs.at[s, 1])
         to_core(half, 3, k)
 
+    def along_z(src, at):
+        s = z_slot(src, at)
+        put(kv.at[z_slot(src)], kv.at[s], rs.at[s, 0], dev(dz=at))
+
+    def half_along_z(src, at, part):
+        s = z_slot(src, at)
+        put(kv.at[z_slot(src), part], kv.at[s, part], rs.at[s, part], dev(dz=at))
+
+    def from_z(src):
+        s = z_slot(src)
+        got(kv.at[s], rs.at[s, 0])
+
+    for d in (1, -1, 2, -2):
+        along_z(0, d)
     to_sides(0, 0)
-    for d in (1, 3, 2):
-        s = slot(0, 0, 0, 4 - d)
-        put(kv.at[own], kv.at[s], rs.at[s, 0], dev(dz=d))
     to_core(0, 0, 0)
 
     def turn(t, carry):
@@ -148,8 +164,6 @@
     for d in range(4):
         pair = pl.ds(2 * ((y + d) % NY), 2)
         back = (4 - d) % 4
-        put(sks.at[pair], sk.at[1, y], rsk.at[1, back], dev(dy=d, far=1))
-        put(svs.at[pair], sv.at[1, y], rsv.at[1, back], dev(dy=d, far=1))
         if d == 0:
             keep(sks.at[pair], sk.at[0, y])
             keep(svs.at[pair], sv.at[0, y])
@@ -172,9 +186,6 @@
                 keep(src, qb.at[hr, 0])
             else:
                 put(src, qb.at[hr, back], rq.at[hr, back], dev(dy=d))
-    for d in (0, 1, 3, 2):
-        s = slot(1, 0, 0, (4 - d) % 4)
-        put(kv.at[own], kv.at[s], rs.at[s, 0], dev(dz=d, far=1))
 
     def unit(u):
         k = min(u, 7 - u) if isinstance(u, int) else jnp.minimum(u, 7 - u)
@@ -268,24 +279,54 @@
                 part = score(t, n, buf, j)
                 mx[t] = part if first else jnp.maximum(mx[t], part)
             return carry
-        lax.fori_loop(0, 4, two, 0)
+        lax.fori_loop(0, 4, two, 0, unroll=True)
 
     first = (zl == 0).astype(jnp.int32)
     last = (zl == NH - 1).astype(jnp.int32)
     ka = 1 + 2 * last
     kb = 3 - first - last
     near = (0, ka, kb, 6 - ka - kb)
-    for n in (1, 2, 3):
-        full(0, 0, 0, near[n])
-        to_sides(0, near[n])
-        to_core(0, 0, near[n])
-        relay(0, near[n - 1])
-    for copy in kept:
+    def spread(half, k):
+        to_sides(half, k)
+        to_core(half, 0, k)
+
+    from_z(-1)
+    from_z(1)
+    spread(0, near[1])
+    for sign in (-1, 1):
+        from_z(2 * sign)
+        along_z(2 * sign, -sign)
+    spread(0, near[2])
+    relay(0, near[0])
+    for sign in (-1, 1):
+        from_z(3 * sign)
+        half_along_z(3 * sign, -sign, (1 + sign) // 2)
+    spread(0, near[3])
+    for copy in kept[:2]:
+        copy.wait()
+    for d in (1, 2, 3):
+        src = (y + d) % NY
+        got(sk.at[0, src], rsk.at[0, d])
+        got(sv.at[0, src], rsv.at[0, d])
+    put(sk.at[0], rk, rsk.at[1, 0], dev(dz=2))
+    put(sv.at[0], rv, rsv.at[1, 0], dev(dz=-2))
+    relay(0, near[1])
+    for copy in kept[2:]:
         copy.wait()
     for d in (1, 3, 2):
         got(qb.at[0, d], rq.at[0, d])
     early(0, True)
+    relay(0, near[2])
+    s = slot(1, 0, 0, 0)
+    got(kv.at[s, 0], rs.at[s, 0])
+    got(kv.at[s, 1], rs.at[s, 1])
     relay(0, near[3])
+    got(rk, rsk.at[1, 0])
+    put(rk, sk.at[1], rsk.at[1, 1], dev(dz=2))
+    got(rv, rsv.at[1, 0])
+    put(rv, sv.at[1], rsv.at[1, 1], dev(dz=-2))
+    for n in range(4):
+        spread(1, n)
     for n in range(4):
         full(0, 0, 1, n)
     early(1)
@@ -293,10 +334,6 @@
         close(0, near[n])
     early(2)
     early(4)
-    for n in range(4):
-        full(1, 0, 0, n)
-        to_sides(1, n)
-        to_core(1, 0, n)
     for n in range(4):
         full(0, 1, 1, n)
         full(0, 2, 1, n)
@@ -306,12 +343,8 @@
     for n in range(4):
         full(0, 3, 1, n)
     early(7)
-    for d in range(4):
-        for zr in range(2):
-            if d > 0 or zr > 0:
-                src = (y + d) % NY
-                got(sk.at[zr, src], rsk.at[zr, d])
-                got(sv.at[zr, src], rsv.at[zr, d])
+    got(sk.at[1], rsk.at[1, 1])
+    got(sv.at[1], rsv.at[1, 1])
     early(8)
     early(9)
     for t in range(8):
@@ -381,6 +414,8 @@
             pltpu.VMEM((2, 4, LOCAL * GQ, HEAD), bf),
             pltpu.VMEM((2, 4, 2, LOCAL, HEAD), bf),
             pltpu.VMEM((2, 4, 2, LOCAL, HEAD), bf),
+            pltpu.VMEM((4, 2, LOCAL, HEAD), bf),
+            pltpu.VMEM((4, 2, LOCAL, HEAD), bf),
             pltpu.VMEM((2, 4, LOCAL, GQ, HEAD), bf),
             pltpu.VMEM((LOCAL * 80, HEAD), f32),
             pltpu.VMEM((LOCAL, HEAD), f32),

time: 87.9 us -> 69.1 us (0.79)
  Pallas kernels: 84.8 us -> 66 us
    pallas_call x1, Pallas kernels: 84.8 us -> 66 us  [shards(): pl.pallas_call(kernel, out_shape=jax.ShapeDtypeStruct((LOCAL, 8, GQ, HEAD...]
where the time goes in v4:
time: 69.1 us; the launch traced here: 68.9 us
  Pallas kernels  66 us (96%)
  local copies, waits for them, and re-layouts  2.26 us (3%)
    pallas_call x1, Pallas kernels, shards(): pl.pallas_call(kernel, out_shape=jax.ShapeDtypeStruct((LOCAL, 8, GQ, HEAD...  66 us
    unnamed x1, local copies, waits for them, and re-layouts  2.26 us

profile of v4, /device:TPU:1, one launch (start us, length us, event | category | flops | bytes accessed | tf_op | source)
XLA Modules:
  0.0 68.9 jit_solution(15929751271296511664)
XLA Ops:
  0.7 66.0 %shard_map.73 = bf16[64,8,8,128]{3,2,1,0:T(8,128)(2,1)} custom-call(bf16[64,10,8,128]{3,2,1,0:T(8,128)(2,1)} %bitcast.7, s32[16,128]{1,0:T(8,128)} %bitcast.10, bf16[256,128]{1,0:T(8,128)(2,1)} %bitcast.8, bf16[128,128]{1,0:T(8,128)(2,1)} %bitcast.9, f32[1,128]{1,0:T(1,128)} %bitcast.11, s32[1]{0:T(128)S(6)} %copy.9.block, f32[336,128]{1,0:T(8,128)} %constant.2.clone.table), custom_call_target="tpu_custom_call" | custom-call | tf_op jit(solution)/shard_map/pallas_call | solution.py:404
  66.7 2.3 %copy.10 = bf16[64,8,8,128]{3,2,1,0:T(8,128)(2,1)} copy(bf16[64,8,8,128]{3,2,1,0:T(8,128)(2,1)} %shard_map.73) | data formatting | bytes 2097152

commit v5 on v4

--- a/solution.py
+++ b/solution.py
@@ -17,6 +17,7 @@
 NT = (((1,), (1,)), ((), ()))
 SPANS = [(512 * n, 512) for n in range(8)] + [(4096, 256), (4352, 256)]
 WIDTH = 4608
+DIRECT = (1, 0)
 
 
 def rope_tables():
@@ -30,9 +31,9 @@
     return jnp.asarray(table.astype(np.float32))
 
 
-def kernel(qkv, codes, books, vcodes, scales, block, table, out,
-           kv, qs, sks, svs, qb, sk, sv, rk, rv, ob, xs, cq, sq, g0, g1, mx,
-           send, rs, rq, rsk, rsv, ro, loc, osend):
+def kernel(raw, codes, books, vcodes, scales, block, table, out,
+           qkv, kv, qs, sks, svs, qb, sk, sv, rk, rv, ob, xs, cq, sq, g0, g1, mx,
+           send, rs, rq, rsk, rsv, ro, loc, osend, load):
     o = lax.axis_index("outer")
     i = lax.axis_index("inner")
     zl, x, c = o // 8, (o // 2) % NX, o % 2
@@ -44,11 +45,14 @@
         outer = (z1 % NH) * 8 + ((x + dx) % NX) * 2 + (c + dc) % 2
         return {"outer": outer, "inner": ((y + dy) % NY) * 2 + z1 // NH}
 
-    peers = [dev(dz=d) for d in (1, -1, 2, -2)] + [dev(dx=1), dev(dx=3), dev(dc=1)]
+    peers = [dev(dz=d) for d in (1, -1, 2, -2)] + [dev(dx=d) for d in (1, 2, 3)] + [dev(dc=1)]
     peers += [dev(dy=d) for d in (1, 2, 3)]
     barrier = pltpu.get_barrier_semaphore()
     for peer in peers:
         pl.semaphore_signal(barrier, inc=1, device_id=peer, device_id_type=pl.DeviceIdType.MESH)
+
+    loading = pltpu.make_async_copy(raw, qkv, load)
+    loading.start()
 
     def slot(half, side, core, k):
         return ((half * 4 + side) * 2 + core) * 4 + k
@@ -110,7 +114,7 @@
 
     def to_sides(half, k):
         src = kv.at[slot(half, 0, 0, k)]
-        for side, dx in ((1, 1), (2, 3)):
+        for side, dx in ((1, 1), (2, 3), (3, 2))[:2 + DIRECT[half]]:
             s = slot(half, side, 0, k)
             put(src, kv.at[s], rs.at[s, 0], dev(dx=dx))
 
@@ -123,13 +127,17 @@
             full(half, side, 0, k)
             s = slot(half, 3, 0, k)
             part = side - 1
-            put(kv.at[slot(half, side, 0, k), part], kv.at[s, part], rs.at[s, part], dev(dx=dx))
+            if not DIRECT[half]:
+                put(kv.at[slot(half, side, 0, k), part], kv.at[s, part], rs.at[s, part], dev(dx=dx))
             to_core(half, side, k)
 
     def close(half, k):
         s = slot(half, 3, 0, k)
-        got(kv.at[s, 0], rs.at[s, 0])
-        got(kv.at[s, 1], rs.at[s, 1])
+        if DIRECT[half]:
+            got(kv.at[s], rs.at[s, 0])
+        else:
+            got(kv.at[s, 0], rs.at[s, 0])
+            got(kv.at[s, 1], rs.at[s, 1])
         to_core(half, 3, k)
 
     def along_z(src, at):
@@ -157,6 +165,7 @@
         xs[pl.ds(pl.multiple_of(t * 80 + 72, 8), 8), :] = rows[9]
         return carry
 
+    loading.wait()
     lax.fori_loop(0, LOCAL, turn, 0, unroll=4)
     for h in range(8):
         sks[h] = xs[pl.ds(64 + h, LOCAL, stride=80), :].astype(jnp.bfloat16)
@@ -273,13 +282,16 @@
             own_copy(t // 2).start()
 
     def early(n, first=False):
-        def two(j, carry):
+        for j in range(4):
             for half, buf in ((0, g0), (1, g1)):
                 t = 4 * half + j
                 part = score(t, n, buf, j)
                 mx[t] = part if first else jnp.maximum(mx[t], part)
-            return carry
-        lax.fori_loop(0, 4, two, 0, unroll=True)
+
+    def later(n, first=False):
+        for j in range(4):
+            part = score(8 + j, n, g0, j)
+            mx[j] = part if first else jnp.maximum(mx[j], part)
 
     first = (zl == 0).astype(jnp.int32)
     last = (zl == NH - 1).astype(jnp.int32)
@@ -311,38 +323,42 @@
     put(sk.at[0], rk, rsk.at[1, 0], dev(dz=2))
     put(sv.at[0], rv, rsv.at[1, 0], dev(dz=-2))
     relay(0, near[1])
+    for n in (1, 2, 3):
+        spread(1, n)
+    relay(0, near[2])
+    relay(0, near[3])
     for copy in kept[2:]:
         copy.wait()
     for d in (1, 3, 2):
         got(qb.at[0, d], rq.at[0, d])
     early(0, True)
-    relay(0, near[2])
     s = slot(1, 0, 0, 0)
     got(kv.at[s, 0], rs.at[s, 0])
     got(kv.at[s, 1], rs.at[s, 1])
-    relay(0, near[3])
+    spread(1, 0)
+    for n in range(4):
+        full(0, 0, 1, n)
+    early(1)
+    for n in range(4):
+        close(0, near[n])
+    early(2)
+    early(4)
     got(rk, rsk.at[1, 0])
     put(rk, sk.at[1], rsk.at[1, 1], dev(dz=2))
     got(rv, rsv.at[1, 0])
     put(rv, sv.at[1], rsv.at[1, 1], dev(dz=-2))
-    for n in range(4):
-        spread(1, n)
-    for n in range(4):
-        full(0, 0, 1, n)
-    early(1)
-    for n in range(4):
-        close(0, near[n])
-    early(2)
-    early(4)
     for n in range(4):
         full(0, 1, 1, n)
         full(0, 2, 1, n)
     early(3)
     early(5)
     early(6)
+    for n in (1, 2, 3):
+        relay(1, n)
     for n in range(4):
         full(0, 3, 1, n)
     early(7)
+    relay(1, 0)
     got(sk.at[1], rsk.at[1, 1])
     got(sv.at[1], rsv.at[1, 1])
     early(8)
@@ -360,28 +376,38 @@
     def opening(j):
         stage(j, g0, j)
 
-        @pl.when(j == 0)
-        def _():
-            relay(1, 0)
-            relay(1, 1)
-
         @pl.when(j == 1)
         def _():
-            relay(1, 2)
-            relay(1, 3)
+            for n in (1, 2, 3):
+                close(1, n)
 
         @pl.when(j == 3)
         def _():
-            for n in range(4):
-                close(1, n)
+            close(1, 0)
 
     loop(0, opening)
-    for side in range(4):
-        for n in range(4):
-            full(1, side, 1, n)
     for d in (1, 3, 2):
         got(qb.at[1, d], rq.at[1, d])
-    loop(4, lambda j: stage(4 + j, g1, j, 8 + j, g0))
+    later(0, True)
+    later(8)
+    later(9)
+    for n in range(4):
+        full(1, 0, 1, n)
+    later(1)
+    later(2)
+    later(4)
+    loop(4, lambda j: stage(4 + j, g1, j))
+    for n in range(4):
+        full(1, 1, 1, n)
+        full(1, 2, 1, n)
+    later(3)
+    later(5)
+    later(6)
+    for n in range(4):
+        full(1, 3, 1, n)
+    later(7)
+    for j in range(4):
+        mx[j] = widest(mx[j])
     loop(8, lambda j: stage(8 + j, g0, j, 12 + j, g1))
     loop(12, lambda j: stage(12 + j, g1, j))
 
@@ -404,9 +430,10 @@
     return pl.pallas_call(
         kernel,
         out_shape=jax.ShapeDtypeStruct((LOCAL, 8, GQ, HEAD), bf),
-        in_specs=[vmem] * 5 + [pl.BlockSpec(memory_space=pltpu.SMEM), vmem],
+        in_specs=[pl.BlockSpec(memory_space=pl.ANY)] + [vmem] * 4 + [pl.BlockSpec(memory_space=pltpu.SMEM), vmem],
         out_specs=pl.BlockSpec(memory_space=pl.ANY),
         scratch_shapes=[
+            pltpu.VMEM((LOCAL, GQ + 2, 8, HEAD), bf),
             pltpu.VMEM((64, 2, BLOCK, HEAD), bf),
             pltpu.VMEM((8, LOCAL * GQ, HEAD), bf),
             pltpu.VMEM((8, LOCAL, HEAD), bf),
@@ -424,7 +451,7 @@
             pltpu.VMEM((4, ROWS, WIDTH), f32),
             pltpu.VMEM((8, ROWS, 128), f32),
             dma((128,)), dma((64, 2)), dma((2, 4)), dma((2, 4)), dma((2, 4)),
-            dma((2, 4)), dma((8,)), dma((8,)),
+            dma((2, 4)), dma((8,)), dma((8,)), dma,
         ],
         compiler_params=pltpu.CompilerParams(
             collective_id=0, has_side_effects=True, vmem_limit_bytes=60 * 2**20),

time: 69.1 us -> 63.5 us (0.919)
  the two profiles are of different devices: /device:TPU:1 before, /device:TPU:38 now
where the time goes in v5:
time: 63.5 us; the launch traced here: 63.3 us
  Pallas kernels  60.4 us (95%)
  local copies, waits for them, and re-layouts  2.26 us (4%)
  between operations  0.66 us (1%)
    pallas_call x1, Pallas kernels, shards(): pl.pallas_call(kernel, out_shape=jax.ShapeDtypeStruct((LOCAL, 8, GQ, HEAD...  60.4 us
    unnamed x1, local copies, waits for them, and re-layouts  2.26 us

profile of v5, /device:TPU:38, one launch (start us, length us, event | category | flops | bytes accessed | tf_op | source)
XLA Modules:
  0.0 63.3 jit_solution(6774661815646308183)
XLA Ops:
  0.7 60.4 %shard_map.73 = bf16[64,8,8,128]{3,2,1,0:T(8,128)(2,1)} custom-call(bf16[64,10,8,128]{3,2,1,0:T(8,128)(2,1)} %bitcast.7, s32[16,128]{1,0:T(8,128)} %bitcast.10, bf16[256,128]{1,0:T(8,128)(2,1)} %bitcast.8, bf16[128,128]{1,0:T(8,128)(2,1)} %bitcast.9, f32[1,128]{1,0:T(1,128)} %bitcast.11, s32[1]{0:T(128)S(6)} %copy.9.block, f32[336,128]{1,0:T(8,128)} %constant.2.clone.table), custom_call_target="tpu_custom_call" | custom-call | tf_op jit(solution)/shard_map/pallas_call | solution.py:430
  61.0 2.3 %copy.10 = bf16[64,8,8,128]{3,2,1,0:T(8,128)(2,1)} copy(bf16[64,8,8,128]{3,2,1,0:T(8,128)(2,1)} %shard_map.73) | data formatting | bytes 2097152

commit v6 on v5

--- a/solution.py
+++ b/solution.py
@@ -314,6 +314,8 @@
         from_z(3 * sign)
         half_along_z(3 * sign, -sign, (1 + sign) // 2)
     spread(0, near[3])
+    for n in (1, 2, 3):
+        spread(1, n)
     for copy in kept[:2]:
         copy.wait()
     for d in (1, 2, 3):
@@ -323,8 +325,6 @@
     put(sk.at[0], rk, rsk.at[1, 0], dev(dz=2))
     put(sv.at[0], rv, rsv.at[1, 0], dev(dz=-2))
     relay(0, near[1])
-    for n in (1, 2, 3):
-        spread(1, n)
     relay(0, near[2])
     relay(0, near[3])
     for copy in kept[2:]:
@@ -351,10 +351,10 @@
         full(0, 1, 1, n)
         full(0, 2, 1, n)
     early(3)
+    for n in (1, 2, 3):
+        relay(1, n)
     early(5)
     early(6)
-    for n in (1, 2, 3):
-        relay(1, n)
     for n in range(4):
         full(0, 3, 1, n)
     early(7)

time: 63.5 us -> 63.5 us (level)
  no operation moved by 1% of the time
where the time goes in v6:
time: 63.5 us; the launch traced here: 63.3 us
  Pallas kernels  60.4 us (95%)
  local copies, waits for them, and re-layouts  2.26 us (4%)
  between operations  0.66 us (1%)
    pallas_call x1, Pallas kernels, shards(): pl.pallas_call(kernel, out_shape=jax.ShapeDtypeStruct((LOCAL, 8, GQ, HEAD...  60.4 us
    unnamed x1, local copies, waits for them, and re-layouts  2.26 us

profile of v6, /device:TPU:38, one launch (start us, length us, event | category | flops | bytes accessed | tf_op | source)
XLA Modules:
  0.0 63.3 jit_solution(381668130486496426)
XLA Ops:
  0.7 60.4 %shard_map.73 = bf16[64,8,8,128]{3,2,1,0:T(8,128)(2,1)} custom-call(bf16[64,10,8,128]{3,2,1,0:T(8,128)(2,1)} %bitcast.7, s32[16,128]{1,0:T(8,128)} %bitcast.10, bf16[256,128]{1,0:T(8,128)(2,1)} %bitcast.8, bf16[128,128]{1,0:T(8,128)(2,1)} %bitcast.9, f32[1,128]{1,0:T(1,128)} %bitcast.11, s32[1]{0:T(128)S(6)} %copy.9.block, f32[336,128]{1,0:T(8,128)} %constant.2.clone.table), custom_call_target="tpu_custom_call" | custom-call | tf_op jit(solution)/shard_map/pallas_call | solution.py:430
  61.0 2.3 %copy.10 = bf16[64,8,8,128]{3,2,1,0:T(8,128)(2,1)} copy(bf16[64,8,8,128]{3,2,1,0:T(8,128)(2,1)} %shard_map.73) | data formatting | bytes 2097152
